TPU v7x, 512 devices: a whole 4x8x8 slice. The times are simulated.
512 devices in a mesh: group: 2 (over y_lo), gx: 32 (over y_hi, z), gy: 8 (over x, core).
Axes of the slice: x: 4, y: 8 (y_hi: 4, y_lo: 2; y = y_hi * 2 + y_lo), z: 8, core: 2. Of those that a mesh axis runs over, the one named last changes fastest.
Arguments:
- les_state: float32 [5, 256, 96, 1024], P(None, 'gx', 'group', 'gy'), may hold values from -0.5 to 1.25, as said below
- wave_state: float32 [3, 256, 2048], P(None, 'gx', ('group', 'gy')), may hold values from -6 to 6
- restriction_ops: bfloat16 [1536, 4, 128], replicated, may hold values from -0.15625 to 0.15625
- pair_owner: int32 [16, 256, 4], P(('group', 'gy'), 'gx'), may hold values from 0 to 31, all different within a row; in each aligned block of 8 rows (0 to 7, 8 to 15, ..., all dimensions but the last counted through in order) at most 2 rows name the same one
- pair_slot: int32 [16, 256, 4], P(('group', 'gy'), 'gx'), may hold values from 0 to 7
- pair_weight: int32 [16, 256, 4], P(('group', 'gy'), 'gx'), may hold values from 0 to 3
- tile_mask: int32 [16, 256], P(('group', 'gy'), 'gx'), may hold values 0 or 1
Outputs:
- les_next: float32 [5, 256, 96, 1024], P(None, 'gx', 'group', 'gy')
- wave_next: float32 [3, 256, 2048], P(None, 'gx', ('group', 'gy'))
Inputs may be any that keep to these rules, and one draw needn't show every extreme that they name: `les_state`: density and pressure lie in 0.75 to 1.25, the velocities in -0.5 to 0.5. `pair_owner`: each tile names 4 different owners; among the tiles of one device at most 2 pairs name the same owner, and some device reaches 2.
All inputs are finite; a program needn't handle non-finite values. No bound on the sum of `tile_mask` on one device may be relied on, other than what follows from the above.
Results may differ from a plain program's by a relative error of at most 0.00075.
Values may be sent and summed in bfloat16 or wider, within the bound.
A program may use at most 64 MiB of HBM per device.

v0:
```python
import jax
import jax.numpy as jnp
from jax import lax
from jax.sharding import PartitionSpec as P

GAMMA = 1.4
VISCOSITY = 0.05
LES_STEP = 0.2
WAVE_STEP = 0.3


def with_halo(block, sides, width, periodic):
    for axis, dim in sides:
        count = lax.axis_size(axis)
        forward = [(i, i + 1) for i in range(count - 1)]
        if periodic:
            forward.append((count - 1, 0))
        backward = [(target, source) for source, target in forward]
        low = lax.ppermute(
            lax.slice_in_dim(block, block.shape[dim] - width, None, axis=dim), axis, forward
        )
        high = lax.ppermute(lax.slice_in_dim(block, 0, width, axis=dim), axis, backward)
        block = jnp.concatenate([low, block, high], axis=dim)
    return block


def window(array_in, offsets, margin):
    picker = tuple(
        (
            slice(margin + shift_by, array_in.shape[axis_id] - margin + shift_by)
            for axis_id, shift_by in enumerate(offsets)
        )
    )
    return array_in[picker]


def shifted(dim_count, axis_id, amount):
    return tuple((amount if which_axis == axis_id else 0 for which_axis in range(dim_count)))


def central_four(array_in, axis_id):
    dim_count = array_in.ndim
    ahead_one = window(array_in, shifted(dim_count, axis_id, 1), 2)
    behind_one = window(array_in, shifted(dim_count, axis_id, -1), 2)
    ahead_two = window(array_in, shifted(dim_count, axis_id, 2), 2)
    behind_two = window(array_in, shifted(dim_count, axis_id, -2), 2)
    return (8.0 * (ahead_one - behind_one) - (ahead_two - behind_two)) / 12.0


def les_tendency(block_in):
    density = block_in[0]
    velocity = (block_in[1], block_in[2], block_in[3])
    pressure = block_in[4]
    middle = (0, 0, 0)
    centred = [window(component, middle, 2) for component in velocity]
    rho_mid = window(density, middle, 2)
    press_mid = window(pressure, middle, 2)
    divergence = (
        central_four(velocity[0], 0) + central_four(velocity[1], 1) + central_four(velocity[2], 2)
    )

    def advect(quantity):
        return (
            centred[0] * central_four(quantity, 0)
            + centred[1] * central_four(quantity, 1)
            + centred[2] * central_four(quantity, 2)
        )

    rate_list = [-advect(density) - rho_mid * divergence]
    for axis_id in range(3):
        component = velocity[axis_id]
        laplace = -6.0 * centred[axis_id]
        for other_axis in range(3):
            laplace = (
                laplace
                + window(component, shifted(3, other_axis, 1), 2)
                + window(component, shifted(3, other_axis, -1), 2)
            )
        rate_list.append(
            -advect(component) - central_four(pressure, axis_id) / rho_mid + VISCOSITY * laplace
        )
    rate_list.append(-advect(pressure) - GAMMA * press_mid * divergence)
    return jnp.stack(rate_list)


def lighthill(block_in):
    density = block_in[0]
    velocity = (block_in[1], block_in[2], block_in[3])
    summed = jnp.zeros(window(density, (0, 0, 0), 2).shape, jnp.float32)
    for row_axis in range(3):
        for col_axis in range(row_axis, 3):
            stress = density * velocity[row_axis] * velocity[col_axis]
            if row_axis == col_axis:
                piece_term = (
                    window(stress, shifted(3, row_axis, 2), 2)
                    - 2.0 * window(stress, (0, 0, 0), 2)
                    + window(stress, shifted(3, row_axis, -2), 2)
                ) / 4.0
            else:
                both_up = tuple(
                    (a + b for a, b in zip(shifted(3, row_axis, 1), shifted(3, col_axis, 1)))
                )
                up_down = tuple(
                    (a + b for a, b in zip(shifted(3, row_axis, 1), shifted(3, col_axis, -1)))
                )
                down_up = tuple(
                    (a + b for a, b in zip(shifted(3, row_axis, -1), shifted(3, col_axis, 1)))
                )
                both_down = tuple(
                    (a + b for a, b in zip(shifted(3, row_axis, -1), shifted(3, col_axis, -1)))
                )
                piece_term = (
                    2.0
                    * (
                        window(stress, both_up, 2)
                        - window(stress, up_down, 2)
                        - window(stress, down_up, 2)
                        + window(stress, both_down, 2)
                    )
                    / 4.0
                )
            summed = summed + piece_term
    return summed


def coarse_tiles(source, mask_row):
    rows_x, depth_z, width_y = source.shape
    halved = source.reshape(rows_x, depth_z // 2, 2, width_y).sum(axis=2)
    halved = halved.reshape(rows_x, depth_z // 2, width_y // 2, 2).sum(axis=3)
    return (halved.reshape(rows_x, -1) * mask_row[:, None]).astype(jnp.bfloat16)


def wave_tendency(block_in, wave_source, radius):
    pressure = block_in[0]
    axial = block_in[1]
    radial = block_in[2]
    radial_mid = window(radial, (0, 0), 2)
    press_rate = (
        wave_source
        - central_four(axial, 0)
        - central_four(radial, 1)
        - radial_mid / radius[None, :]
    )
    return jnp.stack([press_rate, -central_four(pressure, 0), -central_four(pressure, 1)])


def wave_rims(block_in):
    return with_halo(block_in, (("gx", 1), (("group", "gy"), 2)), 2, False)


def on_device(
    les_state, wave_state, restriction_ops, pair_owner, pair_slot, pair_weight, tile_mask
):
    padded = with_halo(les_state, (("group", 2), ("gx", 1), ("gy", 3)), 2, True)
    first_rate = les_tendency(padded)
    predicted = with_halo(
        les_state + LES_STEP * first_rate, (("group", 2), ("gx", 1), ("gy", 3)), 2, True
    )
    second_rate = les_tendency(predicted)
    les_next = les_state + 0.5 * LES_STEP * (first_rate + second_rate)
    tile_rows = coarse_tiles(lighthill(predicted), tile_mask[0].astype(jnp.float32))
    tile_count, tile_len = tile_rows.shape
    op_count = restriction_ops.shape[1]
    line_width = restriction_ops.shape[2]
    op_table = restriction_ops.reshape(tile_len, op_count * line_width)
    fan_out = pair_owner.shape[-1]
    owners = pair_owner.reshape(-1)
    slot_ids = pair_slot.reshape(-1)
    weight_ids = pair_weight.reshape(-1)
    groups = lax.axis_size("gx")
    capacity = 2 * ((tile_count * fan_out + groups - 1) // groups)
    pair_order = jnp.arange(owners.shape[0], dtype=jnp.int32)
    earlier = (owners[:, None] == owners[None, :]) & (pair_order[None, :] < pair_order[:, None])
    slot_target = owners * capacity + jnp.sum(earlier.astype(jnp.int32), axis=1)
    placing = (
        jnp.arange(groups * capacity, dtype=jnp.int32)[:, None] == slot_target[None, :]
    ).astype(jnp.int32)
    line_sent = jnp.sum(placing * slot_ids[None, :], axis=1).reshape(groups, capacity)
    weight_sent = jnp.sum(placing * weight_ids[None, :], axis=1).reshape(groups, capacity)
    tile_of = jnp.sum(placing * (pair_order // fan_out)[None, :], axis=1)
    occupied = jnp.sum(placing, axis=1)
    chooser = (
        (tile_of[:, None] == jnp.arange(tile_count, dtype=jnp.int32)[None, :])
        & (occupied[:, None] > 0)
    ).astype(jnp.bfloat16)
    fine_sent = (
        jnp.dot(chooser, tile_rows, preferred_element_type=jnp.float32)
        .astype(jnp.bfloat16)
        .reshape(groups, capacity, tile_len)
    )
    fine_in = lax.all_to_all(fine_sent, "gx", split_axis=0, concat_axis=0, tiled=True)
    weight_in = lax.all_to_all(weight_sent, "gx", split_axis=0, concat_axis=0, tiled=True)
    line_in = lax.all_to_all(line_sent, "gx", split_axis=0, concat_axis=0, tiled=True)
    products = jnp.dot(fine_in.reshape(-1, tile_len), op_table, preferred_element_type=jnp.float32)
    products = products.reshape(fine_in.shape[0], fine_in.shape[1], op_count, line_width)
    pick_in = (weight_in[:, :, None] == jnp.arange(op_count, dtype=jnp.int32)).astype(jnp.float32)
    arrived = jnp.einsum("gcw,gcwa->gca", pick_in, products, precision=lax.Precision.HIGHEST)
    lines_here = wave_state.shape[1]
    radial_count = wave_state.shape[2]
    line_flat = line_in.reshape(-1)
    gather_lines = (jnp.arange(lines_here, dtype=jnp.int32)[:, None] == line_flat[None, :]).astype(
        jnp.float32
    )
    wave_source = jnp.dot(
        gather_lines, arrived.reshape(-1, line_width), precision=lax.Precision.HIGHEST
    )
    radial_base = (
        lax.axis_index("group") * lax.axis_size("gy") + lax.axis_index("gy")
    ) * radial_count
    radius = (radial_base + jnp.arange(radial_count, dtype=jnp.int32)).astype(jnp.float32) + 0.5
    current = wave_state
    for step_id in range(2):
        first_wave = wave_tendency(wave_rims(current), wave_source, radius)
        second_wave = wave_tendency(
            wave_rims(current + WAVE_STEP * first_wave), wave_source, radius
        )
        current = current + 0.5 * WAVE_STEP * (first_wave + second_wave)
    return (les_next, current)


def solution(mesh):
    return jax.shard_map(
        on_device,
        mesh=mesh,
        in_specs=(
            P(None, "gx", "group", "gy"),
            P(None, "gx", ("group", "gy")),
            P(),
            P(("group", "gy"), "gx", None),
            P(("group", "gy"), "gx", None),
            P(("group", "gy"), "gx", None),
            P(("group", "gy"), "gx"),
        ),
        out_specs=(P(None, "gx", "group", "gy"), P(None, "gx", ("group", "gy"))),
        check_vma=False,
    )
```

profile of v0, /device:TPU:39, one launch (start us, length us, event | category | flops | bytes accessed | tf_op | source)
XLA Modules:
  0.0 251.3 jit_solution(2907931498580081527)
XLA Ops:
  0.6 1.0 fusion.279
  1.7 2.3 collective-permute-start
  4.0 3.0 %collective-permute-start.1 = (f32[5,8,2,128]{3,1,2,0:T(8,128)S(1)}, f32[5,8,2,128]{3,1,2,0:T(8,128)S(1)}, u32[]{:S(2)}, u32[]{:S(2)}) collective-permute-start(f32[5,8,2,128]{3,1,2,0:T(8,128)S(1)} %copy.135), channel_id=1, source_target_pairs={{256,0},{0,256},{257,1},{1,257},{258,2},{2,258},{259,3},{3,259},{2... | collective-permute-start | bytes 122888 | tf_op jit(solution)/shard_map/ppermute | solution.py:22
  11.0 15.3 %all-to-all-start.1 = ((s32[32,1,2]{2,1,0:T(1,128)}), s32[32,1,2]{2,1,0:T(1,128)S(1)}, u32[]{:S(2)}, u32[]{:S(2)}) async-start(s32[32,1,2]{2,1,0:T(1,128)} %bitcast.21), calls=%async_computation.1 | async-start | bytes 32768 | tf_op jit(solution)/shard_map/all_to_all | solution.py:192
  27.1 3.1 %collective-permute-start.12 = (f32[3,2,128]{2,1,0:T(2,128)S(1)}, f32[3,2,128]{2,1,0:T(2,128)S(1)}, u32[]{:S(2)}, u32[]{:S(2)}) collective-permute-start(f32[3,2,128]{2,1,0:T(2,128)S(1)} %get-tuple-element.96), channel_id=1, source_target_pairs={{0,8},{8,16},{16,24},{24,32},{32,40},{40,48},{48,56},{56,64},{64,7... | collective-permute-start | bytes 9224 | tf_op jit(solution)/shard_map/ppermute | solution.py:19
  30.2 6.4 %collective-permute-start.13 = (f32[3,2,128]{2,1,0:T(2,128)S(1)}, f32[3,2,128]{2,1,0:T(2,128)S(1)}, u32[]{:S(2)}, u32[]{:S(2)}) collective-permute-start(f32[3,2,128]{2,1,0:T(2,128)S(1)} %get-tuple-element.97), channel_id=1, source_target_pairs={{8,0},{16,8},{24,16},{32,24},{40,32},{48,40},{56,48},{64,56},{72,6... | collective-permute-start | bytes 9224 | tf_op jit(solution)/shard_map/ppermute | solution.py:22
  36.6 1.5 constant_dynamic-update-slice_fusion.1
  38.4 1.9 collective-permute-start.2
  40.3 7.6 %collective-permute-start.3 = (f32[5,2,52,128]{3,1,2,0:T(2,128)S(1)}, f32[5,2,52,128]{3,1,2,0:T(2,128)S(1)}, u32[]{:S(2)}, u32[]{:S(2)}) collective-permute-start(f32[5,2,52,128]{3,1,2,0:T(2,128)S(1)} %get-tuple-element.57), channel_id=1, source_target_pairs={{8,0},{16,8},{24,16},{32,24},{40,32},{48,40},{56,48},{64,56},{72,6... | collective-permute-start | bytes 798728 | tf_op jit(solution)/shard_map/ppermute | solution.py:22
  49.0 7.1 %collective-permute-done.2 = f32[5,2,52,128]{3,1,2,0:T(2,128)S(1)} collective-permute-done((f32[5,2,52,128]{3,1,2,0:T(2,128)S(1)}, f32[5,2,52,128]{3,1,2,0:T(2,128)S(1)}, u32[]{:S(2)}, u32[]{:S(2)}) %collective-permute-start.2) | collective-permute-done | bytes 266272 | tf_op jit(solution)/shard_map/ppermute | solution.py:19
  57.1 2.1 fusion.276
  59.2 2.9 %copy.91 = f32[5,12,52,2]{2,3,1,0:T(2,128)} copy(f32[5,12,52,2]{3,1,2,0:T(8,128)} %get-tuple-element.52) | data formatting | bytes 49920 | tf_op jit(solution)/shard_map/slice | solution.py:20
  62.2 2.2 collective-permute-start.4
  64.4 1.4 copy.92
  66.3 1.7 copy.136
  68.0 1.8 copy.111
  70.5 1.9 copy.93
  72.4 3.1 %copy.94 = f32[5,12,52,2]{3,1,2,0:T(8,128)} copy(f32[5,12,52,2]{2,3,1,0:T(2,128)} %collective-permute-done.5) | data formatting | bytes 49920 | tf_op jit(solution)/shard_map/ppermute | solution.py:22
  75.5 4.4 %pad_maximum_fusion = f32[5,12,52,132]{3,1,2,0:T(8,128)S(1)} fusion(f32[5,12,52,2]{3,1,2,0:T(8,128)} %copy.94, f32[5,2,52,128]{3,1,2,0:T(2,128)} %copy-done.7, f32[5,8,52,128]{3,1,2,0:T(8,128)S(1)} %constant_dynamic-update-slice_fusion, f32[5,2,52,128]{3,1,2,0:T(2,128)S(1)} %collective-permute-done.2, f32[5,12,52,2]{3,1,2,0:T(8,128)S(1)} %copy.93), kind=kLoop, calls=%fused_computation | loop fusion | flops 1647360 | bytes 3294720 | tf_op jit(solution)/shard_map/concatenate | solution.py:23
  80.7 1.4 fusion.155
  82.0 0.9 fusion.137
  83.0 0.9 fusion.121
  83.9 0.9 fusion.106
  86.2 4.0 %collective-permute-start.6 = (f32[5,8,2,128]{3,1,2,0:T(8,128)S(1)}, f32[5,8,2,128]{3,1,2,0:T(8,128)S(1)}, u32[]{:S(2)}, u32[]{:S(2)}) collective-permute-start(f32[5,8,2,128]{3,1,2,0:T(8,128)S(1)} %get-tuple-element.58), channel_id=1, source_target_pairs={{0,256},{256,0},{1,257},{257,1},{2,258},{258,2},{3,259},{259,3},{4... | collective-permute-start | bytes 122888 | tf_op jit(solution)/shard_map/ppermute | solution.py:19
  90.1 1.9 collective-permute-start.7
  92.1 11.3 %all-to-all-start = ((s32[32,1,2]{2,1,0:T(1,128)}), s32[32,1,2]{2,1,0:T(1,128)S(1)}, u32[]{:S(2)}, u32[]{:S(2)}) async-start(s32[32,1,2]{2,1,0:T(1,128)} %bitcast.20), calls=%async_computation | async-start | bytes 32768 | tf_op jit(solution)/shard_map/all_to_all | solution.py:193
  104.1 5.6 %all-to-all-done = s32[32,1,2]{2,1,0:T(1,128)S(1)} async-done(((s32[32,1,2]{2,1,0:T(1,128)}), s32[32,1,2]{2,1,0:T(1,128)S(1)}, u32[]{:S(2)}, u32[]{:S(2)}) %all-to-all-start) | async-done | bytes 288 | tf_op jit(solution)/shard_map/all_to_all | solution.py:193
  111.6 2.2 collective-permute-start.8
  113.8 7.3 %collective-permute-start.9 = (f32[5,2,52,128]{3,1,2,0:T(2,128)S(1)}, f32[5,2,52,128]{3,1,2,0:T(2,128)S(1)}, u32[]{:S(2)}, u32[]{:S(2)}) collective-permute-start(f32[5,2,52,128]{3,1,2,0:T(2,128)S(1)} %get-tuple-element.55), channel_id=1, source_target_pairs={{8,0},{16,8},{24,16},{32,24},{40,32},{48,40},{56,48},{64,56},{72,6... | collective-permute-start | bytes 798728 | tf_op jit(solution)/shard_map/ppermute | solution.py:22
  121.8 7.3 %collective-permute-start.14 = (f32[3,12,2]{2,1,0:T(8,128)S(1)}, f32[3,12,2]{2,1,0:T(8,128)S(1)}, u32[]{:S(2)}, u32[]{:S(2)}) collective-permute-start(f32[3,12,2]{2,1,0:T(8,128)S(1)} %get-tuple-element.80), channel_id=1, source_target_pairs={{0,1},{1,2},{2,3},{3,4},{4,5},{5,6},{6,7},{7,256},{256,257},{257,2... | collective-permute-start | bytes 872 | tf_op jit(solution)/shard_map/ppermute | solution.py:19
  129.1 2.1 collective-permute-start.15
  132.4 2.1 fusion.275
  134.5 2.9 %copy.96 = f32[5,12,52,2]{2,3,1,0:T(2,128)} copy(f32[5,12,52,2]{3,1,2,0:T(8,128)} %get-tuple-element.50) | data formatting | bytes 49920 | tf_op jit(solution)/shard_map/slice | solution.py:20
  137.4 2.0 collective-permute-start.10
  139.4 1.4 copy.97
  141.6 1.9 copy.98
  143.5 2.4 collective-permute-done.11
  145.9 3.1 %copy.99 = f32[5,12,52,2]{3,1,2,0:T(8,128)} copy(f32[5,12,52,2]{2,3,1,0:T(2,128)} %collective-permute-done.11) | data formatting | bytes 49920 | tf_op jit(solution)/shard_map/ppermute | solution.py:22
  149.0 5.9 %pad_maximum_fusion.1 = f32[5,12,52,132]{3,1,2,0:T(8,128)S(1)} fusion(f32[5,12,52,2]{3,1,2,0:T(8,128)} %copy.99, f32[5,2,52,128]{3,1,2,0:T(2,128)} %copy-done.6, f32[5,8,2,128]{3,1,2,0:T(8,128)S(1)} %collective-permute-done.7, f32[5,8,48,128]{3,1,2,0:T(8,128)S(1)} %multiply_add_fusion.1, f32[5,8,2,128]{3,1,2,0:T(8,128)S(1)} %collective-permute-done.6, ...), kind=kLoop, calls=%fused_computation.1 | loop fusion | flops 2471040 | bytes 3294720 | tf_op jit(solution)/shard_map/concatenate | solution.py:23
  155.6 1.3 copy-done
  157.0 1.1 fusion.1
  159.7 14.1 %all-to-all-start.2 = ((bf16[32,2,1536]{2,1,0:T(2,128)(2,1)}), bf16[32,2,1536]{2,1,0:T(2,128)(2,1)}, u32[]{:S(2)}, u32[]{:S(2)}) async-start(bf16[32,2,1536]{2,1,0:T(2,128)(2,1)} %reshape.88), calls=%async_computation.2 | async-start | bytes 393216 | tf_op jit(solution)/shard_map/all_to_all | solution.py:191
  173.8 3.5 %slice_bitcast_fusion = (f32[12,52,132]{2,0,1:T(8,128)}, f32[12,52,132]{2,0,1:T(8,128)S(1)}, f32[12,52,132]{2,0,1:T(8,128)S(1)}, f32[12,52,132]{2,0,1:T(8,128)S(1)}, f32[12,52,132]{2,0,1:T(8,128)S(1)}) fusion(f32[5,12,52,132]{3,1,2,0:T(8,128)} %copy-done), kind=kLoop, calls=%fused_computation.9 | loop fusion | bytes 3294720 | tf_op jit(solution)/shard_map/squeeze | solution.py:53
  177.4 5.0 %all-to-all-done.2 = bf16[32,2,1536]{2,1,0:T(2,128)(2,1)} async-done(((bf16[32,2,1536]{2,1,0:T(2,128)(2,1)}), bf16[32,2,1536]{2,1,0:T(2,128)(2,1)}, u32[]{:S(2)}, u32[]{:S(2)}) %all-to-all-start.2) | async-done | bytes 196640 | tf_op jit(solution)/shard_map/all_to_all | solution.py:191
  182.4 2.1 fusion.166
  185.2 2.5 collective-permute-start.16
  187.7 7.0 %collective-permute-start.17 = (f32[3,2,128]{2,1,0:T(2,128)S(1)}, f32[3,2,128]{2,1,0:T(2,128)S(1)}, u32[]{:S(2)}, u32[]{:S(2)}) collective-permute-start(f32[3,2,128]{2,1,0:T(2,128)S(1)} %get-tuple-element.95), channel_id=1, source_target_pairs={{8,0},{16,8},{24,16},{32,24},{40,32},{48,40},{56,48},{64,56},{72,6... | collective-permute-start | bytes 9224 | tf_op jit(solution)/shard_map/ppermute | solution.py:22
  194.8 1.4 fusion.79
  196.3 4.6 %collective-permute-start.18 = (f32[3,12,2]{2,1,0:T(8,128)S(1)}, f32[3,12,2]{2,1,0:T(8,128)S(1)}, u32[]{:S(2)}, u32[]{:S(2)}) collective-permute-start(f32[3,12,2]{2,1,0:T(8,128)S(1)} %get-tuple-element.78), channel_id=1, source_target_pairs={{0,1},{1,2},{2,3},{3,4},{4,5},{5,6},{6,7},{7,256},{256,257},{257,2... | collective-permute-start | bytes 872 | tf_op jit(solution)/shard_map/ppermute | solution.py:19
  200.9 2.2 collective-permute-start.19
  203.1 0.9 fusion.61
  204.0 4.1 %collective-permute-done.19 = f32[3,12,2]{2,1,0:T(8,128)S(1)} collective-permute-done((f32[3,12,2]{2,1,0:T(8,128)S(1)}, f32[3,12,2]{2,1,0:T(8,128)S(1)}, u32[]{:S(2)}, u32[]{:S(2)}) %collective-permute-start.19) | collective-permute-done | bytes 320 | tf_op jit(solution)/shard_map/ppermute | solution.py:22
  208.4 1.9 collective-permute-start.20
  210.3 8.0 %collective-permute-start.21 = (f32[3,2,128]{2,1,0:T(2,128)S(1)}, f32[3,2,128]{2,1,0:T(2,128)S(1)}, u32[]{:S(2)}, u32[]{:S(2)}) collective-permute-start(f32[3,2,128]{2,1,0:T(2,128)S(1)} %get-tuple-element.93), channel_id=1, source_target_pairs={{8,0},{16,8},{24,16},{32,24},{40,32},{48,40},{56,48},{64,56},{72,6... | collective-permute-start | bytes 9224 | tf_op jit(solution)/shard_map/ppermute | solution.py:22
  218.3 0.9 fusion.45
  219.4 2.5 %collective-permute-start.22 = (f32[3,12,2]{2,1,0:T(8,128)S(1)}, f32[3,12,2]{2,1,0:T(8,128)S(1)}, u32[]{:S(2)}, u32[]{:S(2)}) collective-permute-start(f32[3,12,2]{2,1,0:T(8,128)S(1)} %get-tuple-element.76), channel_id=1, source_target_pairs={{0,1},{1,2},{2,3},{3,4},{4,5},{5,6},{6,7},{7,256},{256,257},{257,2... | collective-permute-start | bytes 872 | tf_op jit(solution)/shard_map/ppermute | solution.py:19
  221.9 1.9 collective-permute-start.23
  224.8 4.4 %collective-permute-done.23 = f32[3,12,2]{2,1,0:T(8,128)S(1)} collective-permute-done((f32[3,12,2]{2,1,0:T(8,128)S(1)}, f32[3,12,2]{2,1,0:T(8,128)S(1)}, u32[]{:S(2)}, u32[]{:S(2)}) %collective-permute-start.23) | collective-permute-done | bytes 320 | tf_op jit(solution)/shard_map/ppermute | solution.py:22
  229.5 1.9 collective-permute-start.24
  231.4 8.1 %collective-permute-start.25 = (f32[3,2,128]{2,1,0:T(2,128)S(1)}, f32[3,2,128]{2,1,0:T(2,128)S(1)}, u32[]{:S(2)}, u32[]{:S(2)}) collective-permute-start(f32[3,2,128]{2,1,0:T(2,128)S(1)} %get-tuple-element.91), channel_id=1, source_target_pairs={{8,0},{16,8},{24,16},{32,24},{40,32},{48,40},{56,48},{64,56},{72,6... | collective-permute-start | bytes 9224 | tf_op jit(solution)/shard_map/ppermute | solution.py:22
  240.4 2.8 %collective-permute-start.26 = (f32[3,12,2]{2,1,0:T(8,128)S(1)}, f32[3,12,2]{2,1,0:T(8,128)S(1)}, u32[]{:S(2)}, u32[]{:S(2)}) collective-permute-start(f32[3,12,2]{2,1,0:T(8,128)S(1)} %get-tuple-element.74), channel_id=1, source_target_pairs={{0,1},{1,2},{2,3},{3,4},{4,5},{5,6},{6,7},{7,256},{256,257},{257,2... | collective-permute-start | bytes 872 | tf_op jit(solution)/shard_map/ppermute | solution.py:19
  243.1 1.9 collective-permute-start.27
  245.5 1.1 copy.113
  246.6 3.8 %collective-permute-done.27 = f32[3,12,2]{2,1,0:T(8,128)S(1)} collective-permute-done((f32[3,12,2]{2,1,0:T(8,128)S(1)}, f32[3,12,2]{2,1,0:T(8,128)S(1)}, u32[]{:S(2)}, u32[]{:S(2)}) %collective-permute-start.27) | collective-permute-done | bytes 320 | tf_op jit(solution)/shard_map/ppermute | solution.py:22
  (136 shorter events, 22.5 us)
Async XLA Ops:
  0.6 47.8 %copy-start.17 = (s32[1,8]{1,0:T(1,128)S(1)}, s32[1,8]{1,0:T(1,128)}, u32[]{:S(2)}) copy-start(s32[1,8]{1,0:T(1,128)} %param.13) | copy-start | bytes 100
  1.7 34.9 %collective-permute-start = (f32[5,8,2,128]{3,1,2,0:T(8,128)S(1)}, f32[5,8,2,128]{3,1,2,0:T(8,128)S(1)}, u32[]{:S(2)}, u32[]{:S(2)}) collective-permute-start(f32[5,8,2,128]{3,1,2,0:T(8,128)S(1)} %copy.134), channel_id=1, source_target_pairs={{0,256},{256,0},{1,257},{257,1},{2,258},{258,2},{3,259},{259,3},{4... | collective-permute-start | bytes 122888 | tf_op jit(solution)/shard_map/ppermute | solution.py:19
  4.0 34.1 %collective-permute-start.1 = (f32[5,8,2,128]{3,1,2,0:T(8,128)S(1)}, f32[5,8,2,128]{3,1,2,0:T(8,128)S(1)}, u32[]{:S(2)}, u32[]{:S(2)}) collective-permute-start(f32[5,8,2,128]{3,1,2,0:T(8,128)S(1)} %copy.135), channel_id=1, source_target_pairs={{256,0},{0,256},{257,1},{1,257},{258,2},{2,258},{259,3},{3,259},{2... | collective-permute-start | bytes 122888 | tf_op jit(solution)/shard_map/ppermute | solution.py:22
  11.0 81.0 %all-to-all-start.1 = ((s32[32,1,2]{2,1,0:T(1,128)}), s32[32,1,2]{2,1,0:T(1,128)S(1)}, u32[]{:S(2)}, u32[]{:S(2)}) async-start(s32[32,1,2]{2,1,0:T(1,128)} %bitcast.21), calls=%async_computation.1 | async-start | bytes 32768 | tf_op jit(solution)/shard_map/all_to_all | solution.py:192
  27.1 94.0 %collective-permute-start.12 = (f32[3,2,128]{2,1,0:T(2,128)S(1)}, f32[3,2,128]{2,1,0:T(2,128)S(1)}, u32[]{:S(2)}, u32[]{:S(2)}) collective-permute-start(f32[3,2,128]{2,1,0:T(2,128)S(1)} %get-tuple-element.96), channel_id=1, source_target_pairs={{0,8},{8,16},{16,24},{24,32},{32,40},{40,48},{48,56},{56,64},{64,7... | collective-permute-start | bytes 9224 | tf_op jit(solution)/shard_map/ppermute | solution.py:19
  30.2 91.0 %collective-permute-start.13 = (f32[3,2,128]{2,1,0:T(2,128)S(1)}, f32[3,2,128]{2,1,0:T(2,128)S(1)}, u32[]{:S(2)}, u32[]{:S(2)}) collective-permute-start(f32[3,2,128]{2,1,0:T(2,128)S(1)} %get-tuple-element.97), channel_id=1, source_target_pairs={{8,0},{16,8},{24,16},{32,24},{40,32},{48,40},{56,48},{64,56},{72,6... | collective-permute-start | bytes 9224 | tf_op jit(solution)/shard_map/ppermute | solution.py:22
  38.4 17.7 %collective-permute-start.2 = (f32[5,2,52,128]{3,1,2,0:T(2,128)S(1)}, f32[5,2,52,128]{3,1,2,0:T(2,128)S(1)}, u32[]{:S(2)}, u32[]{:S(2)}) collective-permute-start(f32[5,2,52,128]{3,1,2,0:T(2,128)S(1)} %get-tuple-element.56), channel_id=1, source_target_pairs={{0,8},{8,16},{16,24},{24,32},{32,40},{40,48},{48,56},{56,64},{64,7... | collective-permute-start | bytes 798728 | tf_op jit(solution)/shard_map/ppermute | solution.py:19
  40.3 15.8 %collective-permute-start.3 = (f32[5,2,52,128]{3,1,2,0:T(2,128)S(1)}, f32[5,2,52,128]{3,1,2,0:T(2,128)S(1)}, u32[]{:S(2)}, u32[]{:S(2)}) collective-permute-start(f32[5,2,52,128]{3,1,2,0:T(2,128)S(1)} %get-tuple-element.57), channel_id=1, source_target_pairs={{8,0},{16,8},{24,16},{32,24},{40,32},{48,40},{56,48},{64,56},{72,6... | collective-permute-start | bytes 798728 | tf_op jit(solution)/shard_map/ppermute | solution.py:22
  56.1 0.7 copy-start.7
  62.2 8.4 %collective-permute-start.4 = (f32[5,12,52,2]{2,3,1,0:T(2,128)}, f32[5,12,52,2]{2,3,1,0:T(2,128)}, u32[]{:S(2)}, u32[]{:S(2)}) collective-permute-start(f32[5,12,52,2]{2,3,1,0:T(2,128)} %copy.91), channel_id=1, source_target_pairs={{0,1},{1,2},{2,3},{3,4},{4,5},{5,6},{6,7},{7,0},{8,9},{9,10},{10,1... | collective-permute-start | bytes 74888 | tf_op jit(solution)/shard_map/ppermute | solution.py:19
  65.8 6.6 %collective-permute-start.5 = (f32[5,12,52,2]{2,3,1,0:T(2,128)}, f32[5,12,52,2]{2,3,1,0:T(2,128)}, u32[]{:S(2)}, u32[]{:S(2)}) collective-permute-start(f32[5,12,52,2]{2,3,1,0:T(2,128)} %copy.92), channel_id=1, source_target_pairs={{1,0},{2,1},{3,2},{4,3},{5,4},{6,5},{7,6},{0,7},{9,8},{10,9},{11,1... | collective-permute-start | bytes 74888 | tf_op jit(solution)/shard_map/ppermute | solution.py:22
  83.9 1.3 copy-start.2
  85.2 0.9 copy-start.4
  85.2 36.5 %copy-start.8 = (f32[3,8,128]{2,1,0:T(8,128)S(1)}, f32[3,8,128]{2,1,0:T(8,128)}, u32[]{:S(2)}) copy-start(f32[3,8,128]{2,1,0:T(8,128)} %param.8) | copy-start | bytes 36868
  86.2 25.3 %collective-permute-start.6 = (f32[5,8,2,128]{3,1,2,0:T(8,128)S(1)}, f32[5,8,2,128]{3,1,2,0:T(8,128)S(1)}, u32[]{:S(2)}, u32[]{:S(2)}) collective-permute-start(f32[5,8,2,128]{3,1,2,0:T(8,128)S(1)} %get-tuple-element.58), channel_id=1, source_target_pairs={{0,256},{256,0},{1,257},{257,1},{2,258},{258,2},{3,259},{259,3},{4... | collective-permute-start | bytes 122888 | tf_op jit(solution)/shard_map/ppermute | solution.py:19
  90.1 21.3 %collective-permute-start.7 = (f32[5,8,2,128]{3,1,2,0:T(8,128)S(1)}, f32[5,8,2,128]{3,1,2,0:T(8,128)S(1)}, u32[]{:S(2)}, u32[]{:S(2)}) collective-permute-start(f32[5,8,2,128]{3,1,2,0:T(8,128)S(1)} %get-tuple-element.59), channel_id=1, source_target_pairs={{256,0},{0,256},{257,1},{1,257},{258,2},{2,258},{259,3},{3,259},{2... | collective-permute-start | bytes 122888 | tf_op jit(solution)/shard_map/ppermute | solution.py:22
  92.1 17.6 %all-to-all-start = ((s32[32,1,2]{2,1,0:T(1,128)}), s32[32,1,2]{2,1,0:T(1,128)S(1)}, u32[]{:S(2)}, u32[]{:S(2)}) async-start(s32[32,1,2]{2,1,0:T(1,128)} %bitcast.20), calls=%async_computation | async-start | bytes 32768 | tf_op jit(solution)/shard_map/all_to_all | solution.py:193
  111.6 19.6 %collective-permute-start.8 = (f32[5,2,52,128]{3,1,2,0:T(2,128)S(1)}, f32[5,2,52,128]{3,1,2,0:T(2,128)S(1)}, u32[]{:S(2)}, u32[]{:S(2)}) collective-permute-start(f32[5,2,52,128]{3,1,2,0:T(2,128)S(1)} %get-tuple-element.54), channel_id=1, source_target_pairs={{0,8},{8,16},{16,24},{24,32},{32,40},{40,48},{48,56},{56,64},{64,7... | collective-permute-start | bytes 798728 | tf_op jit(solution)/shard_map/ppermute | solution.py:19
  113.8 17.4 %collective-permute-start.9 = (f32[5,2,52,128]{3,1,2,0:T(2,128)S(1)}, f32[5,2,52,128]{3,1,2,0:T(2,128)S(1)}, u32[]{:S(2)}, u32[]{:S(2)}) collective-permute-start(f32[5,2,52,128]{3,1,2,0:T(2,128)S(1)} %get-tuple-element.55), channel_id=1, source_target_pairs={{8,0},{16,8},{24,16},{32,24},{40,32},{48,40},{56,48},{64,56},{72,6... | collective-permute-start | bytes 798728 | tf_op jit(solution)/shard_map/ppermute | solution.py:22
  121.2 0.6 copy-start.10
  121.8 18.9 %collective-permute-start.14 = (f32[3,12,2]{2,1,0:T(8,128)S(1)}, f32[3,12,2]{2,1,0:T(8,128)S(1)}, u32[]{:S(2)}, u32[]{:S(2)}) collective-permute-start(f32[3,12,2]{2,1,0:T(8,128)S(1)} %get-tuple-element.80), channel_id=1, source_target_pairs={{0,1},{1,2},{2,3},{3,4},{4,5},{5,6},{6,7},{7,256},{256,257},{257,2... | collective-permute-start | bytes 872 | tf_op jit(solution)/shard_map/ppermute | solution.py:19
  129.1 11.7 %collective-permute-start.15 = (f32[3,12,2]{2,1,0:T(8,128)S(1)}, f32[3,12,2]{2,1,0:T(8,128)}, u32[]{:S(2)}, u32[]{:S(2)}) collective-permute-start(f32[3,12,2]{2,1,0:T(8,128)S(1)} %get-tuple-element.81), channel_id=1, source_target_pairs={{1,0},{2,1},{3,2},{4,3},{5,4},{6,5},{7,6},{256,7},{257,256},{258,2... | collective-permute-start | bytes 872 | tf_op jit(solution)/shard_map/ppermute | solution.py:22
  131.3 0.7 copy-start.6
  134.5 6.3 %copy-start.11 = (f32[3,2,128]{2,1,0:T(2,128)S(1)}, f32[3,2,128]{2,1,0:T(2,128)}, u32[]{:S(2)}) copy-start(f32[3,2,128]{2,1,0:T(2,128)} %copy-done.10) | copy-start | bytes 9220
  137.4 4.2 %collective-permute-start.10 = (f32[5,12,52,2]{2,3,1,0:T(2,128)}, f32[5,12,52,2]{2,3,1,0:T(2,128)}, u32[]{:S(2)}, u32[]{:S(2)}) collective-permute-start(f32[5,12,52,2]{2,3,1,0:T(2,128)} %copy.96), channel_id=1, source_target_pairs={{0,1},{1,2},{2,3},{3,4},{4,5},{5,6},{6,7},{7,0},{8,9},{9,10},{10,1... | collective-permute-start | bytes 74888 | tf_op jit(solution)/shard_map/ppermute | solution.py:19
  140.8 5.2 %collective-permute-start.11 = (f32[5,12,52,2]{2,3,1,0:T(2,128)}, f32[5,12,52,2]{2,3,1,0:T(2,128)}, u32[]{:S(2)}, u32[]{:S(2)}) collective-permute-start(f32[5,12,52,2]{2,3,1,0:T(2,128)} %copy.97), channel_id=1, source_target_pairs={{1,0},{2,1},{3,2},{4,3},{5,4},{6,5},{7,6},{0,7},{9,8},{10,9},{11,1... | collective-permute-start | bytes 74888 | tf_op jit(solution)/shard_map/ppermute | solution.py:22
  154.9 2.0 copy-start
  158.0 0.6 copy-start.14
  158.1 0.7 copy-start.15
  158.1 0.7 copy-start.16
  159.7 22.7 %all-to-all-start.2 = ((bf16[32,2,1536]{2,1,0:T(2,128)(2,1)}), bf16[32,2,1536]{2,1,0:T(2,128)(2,1)}, u32[]{:S(2)}, u32[]{:S(2)}) async-start(bf16[32,2,1536]{2,1,0:T(2,128)(2,1)} %reshape.88), calls=%async_computation.2 | async-start | bytes 393216 | tf_op jit(solution)/shard_map/all_to_all | solution.py:191
  173.8 10.7 %copy-start.9 = (pred[32,2,4,1]{2,1,0,3:T(4,128)(4,1)S(1)}, pred[32,2,4,1]{2,1,0,3:T(4,128)(4,1)}, u32[]{:S(2)}) copy-start(pred[32,2,4,1]{2,1,0,3:T(4,128)(4,1)} %compare_bitcast_fusion) | copy-start | bytes 772
  177.4 7.6 %copy-start.13 = (s32[64]{0:T(128)S(1)}, s32[64]{0:T(128)}, u32[]{:S(2)}) copy-start(s32[64]{0:T(128)} %eq.76) | copy-start | bytes 772
  177.4 7.7 %copy-start.12 = (f32[128]{0:T(128)S(1)}, f32[128]{0:T(128)}, u32[]{:S(2)}) copy-start(f32[128]{0:T(128)} %convert_add_fusion) | copy-start | bytes 1540
  185.2 10.9 %collective-permute-start.16 = (f32[3,2,128]{2,1,0:T(2,128)S(1)}, f32[3,2,128]{2,1,0:T(2,128)S(1)}, u32[]{:S(2)}, u32[]{:S(2)}) collective-permute-start(f32[3,2,128]{2,1,0:T(2,128)S(1)} %get-tuple-element.94), channel_id=1, source_target_pairs={{0,8},{8,16},{16,24},{24,32},{32,40},{40,48},{48,56},{56,64},{64,7... | collective-permute-start | bytes 9224 | tf_op jit(solution)/shard_map/ppermute | solution.py:19
  187.7 8.4 %collective-permute-start.17 = (f32[3,2,128]{2,1,0:T(2,128)S(1)}, f32[3,2,128]{2,1,0:T(2,128)S(1)}, u32[]{:S(2)}, u32[]{:S(2)}) collective-permute-start(f32[3,2,128]{2,1,0:T(2,128)S(1)} %get-tuple-element.95), channel_id=1, source_target_pairs={{8,0},{16,8},{24,16},{32,24},{40,32},{48,40},{56,48},{64,56},{72,6... | collective-permute-start | bytes 9224 | tf_op jit(solution)/shard_map/ppermute | solution.py:22
  194.8 8.3 %copy-start.1 = (f32[12,52,132]{2,0,1:T(8,128)S(1)}, f32[12,52,132]{2,0,1:T(8,128)}, u32[]{:S(2)}) copy-start(f32[12,52,132]{2,0,1:T(8,128)} %get-tuple-element.40) | copy-start | bytes 988420
  196.3 7.7 %collective-permute-start.18 = (f32[3,12,2]{2,1,0:T(8,128)S(1)}, f32[3,12,2]{2,1,0:T(8,128)S(1)}, u32[]{:S(2)}, u32[]{:S(2)}) collective-permute-start(f32[3,12,2]{2,1,0:T(8,128)S(1)} %get-tuple-element.78), channel_id=1, source_target_pairs={{0,1},{1,2},{2,3},{3,4},{4,5},{5,6},{6,7},{7,256},{256,257},{257,2... | collective-permute-start | bytes 872 | tf_op jit(solution)/shard_map/ppermute | solution.py:19
  200.9 7.3 %collective-permute-start.19 = (f32[3,12,2]{2,1,0:T(8,128)S(1)}, f32[3,12,2]{2,1,0:T(8,128)S(1)}, u32[]{:S(2)}, u32[]{:S(2)}) collective-permute-start(f32[3,12,2]{2,1,0:T(8,128)S(1)} %get-tuple-element.79), channel_id=1, source_target_pairs={{1,0},{2,1},{3,2},{4,3},{5,4},{6,5},{7,6},{256,7},{257,256},{258,2... | collective-permute-start | bytes 872 | tf_op jit(solution)/shard_map/ppermute | solution.py:22
  208.4 10.9 %collective-permute-start.20 = (f32[3,2,128]{2,1,0:T(2,128)S(1)}, f32[3,2,128]{2,1,0:T(2,128)S(1)}, u32[]{:S(2)}, u32[]{:S(2)}) collective-permute-start(f32[3,2,128]{2,1,0:T(2,128)S(1)} %get-tuple-element.92), channel_id=1, source_target_pairs={{0,8},{8,16},{16,24},{24,32},{32,40},{40,48},{48,56},{56,64},{64,7... | collective-permute-start | bytes 9224 | tf_op jit(solution)/shard_map/ppermute | solution.py:19
  210.3 9.0 %collective-permute-start.21 = (f32[3,2,128]{2,1,0:T(2,128)S(1)}, f32[3,2,128]{2,1,0:T(2,128)S(1)}, u32[]{:S(2)}, u32[]{:S(2)}) collective-permute-start(f32[3,2,128]{2,1,0:T(2,128)S(1)} %get-tuple-element.93), channel_id=1, source_target_pairs={{8,0},{16,8},{24,16},{32,24},{40,32},{48,40},{56,48},{64,56},{72,6... | collective-permute-start | bytes 9224 | tf_op jit(solution)/shard_map/ppermute | solution.py:22
  219.4 5.4 %collective-permute-start.22 = (f32[3,12,2]{2,1,0:T(8,128)S(1)}, f32[3,12,2]{2,1,0:T(8,128)S(1)}, u32[]{:S(2)}, u32[]{:S(2)}) collective-permute-start(f32[3,12,2]{2,1,0:T(8,128)S(1)} %get-tuple-element.76), channel_id=1, source_target_pairs={{0,1},{1,2},{2,3},{3,4},{4,5},{5,6},{6,7},{7,256},{256,257},{257,2... | collective-permute-start | bytes 872 | tf_op jit(solution)/shard_map/ppermute | solution.py:19
  221.9 7.3 %collective-permute-start.23 = (f32[3,12,2]{2,1,0:T(8,128)S(1)}, f32[3,12,2]{2,1,0:T(8,128)S(1)}, u32[]{:S(2)}, u32[]{:S(2)}) collective-permute-start(f32[3,12,2]{2,1,0:T(8,128)S(1)} %get-tuple-element.77), channel_id=1, source_target_pairs={{1,0},{2,1},{3,2},{4,3},{5,4},{6,5},{7,6},{256,7},{257,256},{258,2... | collective-permute-start | bytes 872 | tf_op jit(solution)/shard_map/ppermute | solution.py:22
  224.8 20.3 %copy-start.3 = (f32[5,8,48,128]{3,2,1,0:T(8,128)S(1)}, f32[5,8,48,128]{3,2,1,0:T(8,128)}, u32[]{:S(2)}) copy-start(f32[5,8,48,128]{3,2,1,0:T(8,128)} %param.7) | copy-start | bytes 2949124
  224.8 20.3 %copy-start.5 = (f32[5,8,48,128]{3,1,2,0:T(8,128)S(1)}, f32[5,8,48,128]{3,1,2,0:T(8,128)}, u32[]{:S(2)}) copy-start(f32[5,8,48,128]{3,1,2,0:T(8,128)} %copy-done.4) | copy-start | bytes 2949124
  229.5 10.3 %collective-permute-start.24 = (f32[3,2,128]{2,1,0:T(2,128)S(1)}, f32[3,2,128]{2,1,0:T(2,128)S(1)}, u32[]{:S(2)}, u32[]{:S(2)}) collective-permute-start(f32[3,2,128]{2,1,0:T(2,128)S(1)} %get-tuple-element.90), channel_id=1, source_target_pairs={{0,8},{8,16},{16,24},{24,32},{32,40},{40,48},{48,56},{56,64},{64,7... | collective-permute-start | bytes 9224 | tf_op jit(solution)/shard_map/ppermute | solution.py:19
  231.4 8.9 %collective-permute-start.25 = (f32[3,2,128]{2,1,0:T(2,128)S(1)}, f32[3,2,128]{2,1,0:T(2,128)S(1)}, u32[]{:S(2)}, u32[]{:S(2)}) collective-permute-start(f32[3,2,128]{2,1,0:T(2,128)S(1)} %get-tuple-element.91), channel_id=1, source_target_pairs={{8,0},{16,8},{24,16},{32,24},{40,32},{48,40},{56,48},{64,56},{72,6... | collective-permute-start | bytes 9224 | tf_op jit(solution)/shard_map/ppermute | solution.py:22
  240.4 6.3 %collective-permute-start.26 = (f32[3,12,2]{2,1,0:T(8,128)S(1)}, f32[3,12,2]{2,1,0:T(8,128)S(1)}, u32[]{:S(2)}, u32[]{:S(2)}) collective-permute-start(f32[3,12,2]{2,1,0:T(8,128)S(1)} %get-tuple-element.74), channel_id=1, source_target_pairs={{0,1},{1,2},{2,3},{3,4},{4,5},{5,6},{6,7},{7,256},{256,257},{257,2... | collective-permute-start | bytes 872 | tf_op jit(solution)/shard_map/ppermute | solution.py:19
  243.1 7.3 %collective-permute-start.27 = (f32[3,12,2]{2,1,0:T(8,128)S(1)}, f32[3,12,2]{2,1,0:T(8,128)S(1)}, u32[]{:S(2)}, u32[]{:S(2)}) collective-permute-start(f32[3,12,2]{2,1,0:T(8,128)S(1)} %get-tuple-element.75), channel_id=1, source_target_pairs={{1,0},{2,1},{3,2},{4,3},{5,4},{6,5},{7,6},{256,7},{257,256},{258,2... | collective-permute-start | bytes 872 | tf_op jit(solution)/shard_map/ppermute | solution.py:22
where the time goes:
time: 253 us; the launch traced here: 251 us
  starting transfers between devices  139 us (55%)
  local copies, waits for them, and re-layouts  45.7 us (18%)
  waiting for transfers between devices  32.9 us (13%)
  other arithmetic  29 us (11%)
  matrix products  2.9 us (1%)
    ppermute x14, starting transfers between devices, with_halo(): lax.ppermute(lax.slice_in_dim(block, 0, width, axis=dim), axis, backward)  57.5 us
    ppermute x14, starting transfers between devices, with_halo(): lax.ppermute(lax.slice_in_dim(block, block.shape[dim] - width, None, axis...  41.1 us
    all_to_all x1, starting transfers between devices, on_device(): lax.all_to_all(weight_sent, 'gx', split_axis=0, concat_axis=0, tiled=True)  15.3 us
    ppermute x14, waiting for transfers between devices, with_halo(): lax.ppermute(lax.slice_in_dim(block, 0, width, axis=dim), axis, backward)  15.1 us
    all_to_all x1, starting transfers between devices, on_device(): lax.all_to_all(fine_sent, 'gx', split_axis=0, concat_axis=0, tiled=True)  14.1 us
    concatenate x12, other arithmetic, with_halo(): block = jnp.concatenate([low, block, high], axis=dim)  12.2 us
    all_to_all x1, starting transfers between devices, on_device(): lax.all_to_all(line_sent, 'gx', split_axis=0, concat_axis=0, tiled=True)  11.3 us
    slice x14, local copies, waits for them, and re-layouts, with_halo(): lax.slice_in_dim(block, block.shape[dim] - width, None, axis=dim)  11.3 us
  transfers between devices with their start and end apart: 31, of which 8 were waited for; matrix products, arithmetic and copies ran while one was open for 22% of the time, Pallas kernels for 0%

commit v1 on v0

v1 whole, which is shorter than its diff:
```python
import functools

import jax
import jax.numpy as jnp
from jax import lax
from jax.experimental import pallas as pl
from jax.experimental.pallas import tpu as pltpu
from jax.sharding import PartitionSpec as P

MESH = pl.DeviceIdType.MESH
VISCOSITY = 0.05
LES_STEP = 0.2
WAVE_STEP = 0.3
CX, CZ, CY = 8, 48, 128
ZT = CZ // 8
OFFSETS = (1.0, 0.0, 0.0, 0.0, 1.0)
STATE_SCALE = (130816.0, 65408.0, 65408.0, 65408.0, 130816.0)
PRED_SCALE = (24576.0,) * 5


def encode(value, offset, scale):
    return ((value - offset) * scale + 32768.5).astype(jnp.int32)


def decode(code, offset, scale):
    return code.astype(jnp.float32) * (1.0 / scale) + (offset - 32768.0 / scale)


def pair_words(first, second, offset, scale):
    return (encode(first, offset, scale) << 16) | encode(second, offset, scale)


def split_words(words, offset, scale):
    first = decode(lax.shift_right_logical(words, 16), offset, scale)
    return first, decode(words & 0xFFFF, offset, scale)


def lanes():
    return lax.broadcasted_iota(jnp.int32, (8, 128), 1)


def rows():
    return lax.broadcasted_iota(jnp.int32, (8, 128), 0)


def roll_lane(tile, shift):
    shift = shift % tile.shape[1]
    return pltpu.roll(tile, shift, 1) if shift else tile


def roll_row(tile, shift):
    shift = shift % tile.shape[0]
    return pltpu.roll(tile, shift, 0) if shift else tile


def y_shifts(tile, low, high, slot, reach):
    lane = lanes()
    low, high = roll_lane(low, 126 - 2 * slot), roll_lane(high, -2 * slot)
    shifts = []
    for s in reach:
        before = roll_lane(jnp.where(lane >= 128 - s, low, tile), s)
        after = roll_lane(jnp.where(lane < s, high, tile), -s)
        shifts.append((before, after))
    return shifts


def rate_tile(buf, x, zt, low, high):
    base = 8 + 8 * zt

    def at(f, dx, dz):
        return buf[f, x + (2 + dx), pl.ds(base + dz, 8), :]

    centre, grads, laps = [], [], []
    for f in range(5):
        c = at(f, 0, 0)
        xm1, xp1, zm1, zp1 = at(f, -1, 0), at(f, 1, 0), at(f, 0, -1), at(f, 0, 1)
        (ym1, yp1), (ym2, yp2) = y_shifts(c, low, high, f * ZT + zt, (1, 2))
        dx = 8.0 * (xp1 - xm1) - (at(f, 2, 0) - at(f, -2, 0))
        dz = 8.0 * (zp1 - zm1) - (at(f, 0, 2) - at(f, 0, -2))
        dy = 8.0 * (yp1 - ym1) - (yp2 - ym2)
        centre.append(c)
        grads.append((dx, dz, dy))
        laps.append(((xm1 + xp1) + (zm1 + zp1)) + (ym1 + yp1) - 6.0 * c if 1 <= f <= 3 else None)
    rho, u0, u1, u2, p = centre
    div = grads[1][0] + grads[2][1] + grads[3][2]
    inverse = 1.0 / rho

    def advect(f):
        return u0 * grads[f][0] + u1 * grads[f][1] + u2 * grads[f][2]

    twelfth = -1.0 / 12.0
    rates = [(advect(0) + rho * div) * twelfth]
    for d in range(3):
        rates.append((advect(1 + d) + grads[4][d] * inverse) * twelfth + VISCOSITY * laps[1 + d])
    rates.append((advect(4) + 1.4 * (p * div)) * twelfth)
    return centre, rates


def packed_products(tile):
    momentum = tile * roll_lane(tile, -36)
    return (
        momentum * roll_lane(tile, -12),
        momentum * roll_lane(tile, -24),
        momentum * roll_lane(tile, -36),
    )


def wave_rates(state, source, inverse_radius):
    p, ux, ur = state

    def d(f, axis):
        size = f.shape[axis]
        one = pltpu.roll(f, size - 1, axis) - pltpu.roll(f, 1, axis)
        two = pltpu.roll(f, size - 2, axis) - pltpu.roll(f, 2, axis)
        return (8.0 * one - two) * (1.0 / 12.0)

    return (source - d(ux, 0) - d(ur, 1) - ur * inverse_radius, -d(p, 0), -d(p, 1))


def kernel(
    sizes, far_order,
    les_ref, wave_ref, ops_ref, owner_ref, slot_ref, weight_ref, mask_ref,
    les_out, wave_out,
    state, pred, base_sum, s00, s11, s22, s01, s02, s12,
    xs1, xr1, xs2, xr2, zs1, zr1, zs2, zr2, ys1, yr1, ys2, yr2,
    exz_s, exz_r, ezy_s, ezy_r, ezy_x,
    light, ops_raw, ops_wide, ops_mat, spread, weight_tiles,
    sent, received, own_source, near_source, near_wave,
    local_sems, send1, recv1, send2, recv2, wave_send, wave_recv, all_send, all_recv, src_send, src_recv, gossip,
):
    n_group, n_gx, n_gy = sizes
    g, gx, gy = lax.axis_index("group"), lax.axis_index("gx"), lax.axis_index("gy")
    rank = g * n_gy + gy
    n_rank = n_group * n_gy
    gx_low, gx_high = lax.rem(gx + (n_gx - 1), n_gx), lax.rem(gx + 1, n_gx)
    gy_low, gy_high = lax.rem(gy + (n_gy - 1), n_gy), lax.rem(gy + 1, n_gy)
    other = 1 - g
    lane, row = lanes(), rows()

    def remote(src, dst, send_sem, recv_sem, device):
        return pltpu.make_async_remote_copy(
            src_ref=src, dst_ref=dst, send_sem=send_sem, recv_sem=recv_sem, device_id=device, device_id_type=MESH
        )

    barrier = pltpu.get_barrier_semaphore()
    for device in ((g, gx_low, gy), (g, gx_high, gy), (other, gx, gy), (g, gx, gy_low), (g, gx, gy_high)):
        pl.semaphore_signal(barrier, inc=1, device_id=device, device_id_type=MESH)

    load_les = pltpu.make_async_copy(les_ref, state.at[:, 2:10, 8:56, :], local_sems.at[0])
    load_les.start()
    load_ops = pltpu.make_async_copy(ops_ref, ops_raw, local_sems.at[1])
    load_ops.start()
    load_les.wait()

    def gossip_send(r):
        if r < gossip.shape[0]:
            d = 1 << r
            for target in (lax.rem(gx + d, n_gx), lax.rem(gx + (n_gx - d), n_gx)):
                pl.semaphore_signal(gossip.at[r], inc=1, device_id=(g, target, gy), device_id_type=MESH)

    def gossip_wait(r):
        if r < gossip.shape[0]:
            pl.semaphore_wait(gossip.at[r], 2)

    def x_pack(buf, out, scales, layer):
        for f in range(5):
            for side, first in ((0, 2), (1, 8)):
                out[side, f] = pair_words(
                    buf[f, first, 8:56, :], buf[f, first + 1, 8:56, :], OFFSETS[f], scales[f]
                )

    def x_unpack(buf, words, scales):
        for f in range(5):
            for side, first in ((0, 0), (1, 10)):
                one, two = split_words(words[side, f], OFFSETS[f], scales[f])
                buf[f, first, 8:56, :] = one
                buf[f, first + 1, 8:56, :] = two

    def ends(buf, f, x):
        return jnp.where(row < 4, buf[f, x + 2, 8:16, :], buf[f, x + 2, 48:56, :])

    def z_pack(buf, out, scales):
        for f in range(5):
            for j in range(2):
                a = pair_words(ends(buf, f, 2 * j), ends(buf, f, 2 * j + 4), OFFSETS[f], scales[f])
                b = pair_words(ends(buf, f, 2 * j + 1), ends(buf, f, 2 * j + 5), OFFSETS[f], scales[f])
                out[2 * f + j] = jnp.where((row < 2) | (row >= 6), a, roll_row(b, 4))

    def z_unpack(buf, words, scales):
        for f in range(5):
            for j in range(2):
                word = words[2 * f + j]
                for i, part in enumerate((word, roll_row(word, 4))):
                    for x, tile in zip((2 * j + i, 2 * j + i + 4), split_words(part, OFFSETS[f], scales[f])):
                        buf[f, x + 2, 0:8, :] = tile
                        buf[f, x + 2, 56:64, :] = tile

    def y_add(packed, tile, slot):
        here = (lane >> 1) == slot
        return (
            jnp.where(here, roll_lane(tile, 2 * slot), packed[0]),
            jnp.where(here, roll_lane(tile, 2 * slot + 2), packed[1]),
        )

    def y_pack(x, carry):
        packed = (jnp.zeros((8, 128), jnp.float32),) * 2
        for f in range(5):
            for zt in range(ZT):
                packed = y_add(packed, state[f, x + 2, pl.ds(8 + 8 * zt, 8), :], f * ZT + zt)
        ys1[0, x] = packed[0]
        ys1[1, x] = packed[1]
        return carry

    x_pack(state, xs1, STATE_SCALE, 0)
    pl.semaphore_wait(barrier, 5)
    gossip_send(0)
    first = [
        remote(xs1.at[0], xr1.at[1], send1.at[0], recv1.at[1], (g, gx_low, gy)),
        remote(xs1.at[1], xr1.at[0], send1.at[1], recv1.at[0], (g, gx_high, gy)),
        remote(zs1, zr1, send1.at[2], recv1.at[2], (other, gx, gy)),
        remote(ys1.at[0], yr1.at[1], send1.at[3], recv1.at[4], (g, gx, gy_low)),
        remote(ys1.at[1], yr1.at[0], send1.at[4], recv1.at[3], (g, gx, gy_high)),
    ]
    first[0].start()
    first[1].start()
    z_pack(state, zs1, STATE_SCALE)
    first[2].start()
    lax.fori_loop(0, CX, y_pack, 0)
    first[3].start()
    first[4].start()

    load_ops.wait()

    def widen(i, carry):
        part = pl.ds(pl.multiple_of(i * 512, 512), 512)
        ops_wide[...] = ops_raw[part, :].astype(jnp.float32)
        for w in range(4):
            ops_mat[pl.ds(pl.multiple_of(i * 128, 128), 128), w * 128:(w + 1) * 128] = (
                ops_wide[pl.ds(w, 128, stride=4), :].astype(jnp.bfloat16)
            )
        return carry

    lax.fori_loop(0, 12, widen, 0)
    target = jnp.full((8, 128), -1, jnp.int32)
    for k in range(4):
        weights = jnp.zeros((8, 128), jnp.int32)
        for x in range(8):
            line = owner_ref[0, k, x] * 8 + slot_ref[0, k, x]
            target = jnp.where(((lane & 31) == k * 8 + x) & (lane < 96), line, target)
            weights = jnp.where(row == x, weight_ref[0, k, x], weights)
        weight_tiles[k] = weights
    for o in range(n_gx):
        spread[o * 8:(o + 1) * 8, :] = jnp.where(target == row + o * 8, 1.0, 0.0)

    gossip_wait(0)
    gossip_send(1)
    first[2].wait_recv()
    z_unpack(state, zr1, STATE_SCALE)
    first[3].wait_recv()
    first[4].wait_recv()

    def first_rate(x, carry):
        low, high = yr1[0, x], yr1[1, x]
        packed = (jnp.zeros((8, 128), jnp.float32),) * 2
        for zt in range(ZT):
            centre, rates = rate_tile(state, x, zt, low, high)
            part = pl.ds(8 * zt, 8)
            inner = pl.ds(8 + 8 * zt, 8)
            new = []
            for f in range(5):
                value = centre[f] + LES_STEP * rates[f]
                pred[f, x + 2, inner, :] = value
                base_sum[f, x, part, :] = centre[f] + (0.5 * LES_STEP) * rates[f]
                packed = y_add(packed, value, f * ZT + zt)
                new.append(value)
            rho, u0, u1, u2, _ = new
            m0, m1 = rho * u0, rho * u1
            s00[x + 2, part, :] = m0 * u0
            s01[x + 1, inner, :] = m0 * u1
            s02[x + 1, part, :] = m0 * u2
            s11[x, inner, :] = m1 * u1
            s12[x, inner, :] = m1 * u2
            s22[x, part, :] = rho * u2 * u2
        ys2[0, x] = packed[0]
        ys2[1, x] = packed[1]
        return carry

    lax.fori_loop(2, 6, first_rate, 0)
    gossip_wait(1)
    gossip_send(2)
    first[0].wait_recv()
    first[1].wait_recv()
    x_unpack(state, xr1, STATE_SCALE)
    lax.fori_loop(0, 4, lambda j, carry: first_rate(lax.rem(j + 6, 8), carry), 0)

    x_pack(pred, xs2, PRED_SCALE, 0)
    second = [
        remote(xs2.at[0], xr2.at[1], send2.at[0], recv2.at[1], (g, gx_low, gy)),
        remote(xs2.at[1], xr2.at[0], send2.at[1], recv2.at[0], (g, gx_high, gy)),
        remote(zs2, zr2, send2.at[2], recv2.at[2], (other, gx, gy)),
        remote(ys2.at[0], yr2.at[1, 1:9], send2.at[3], recv2.at[4], (g, gx, gy_low)),
        remote(ys2.at[1], yr2.at[0, 1:9], send2.at[4], recv2.at[3], (g, gx, gy_high)),
        remote(ezy_s.at[0], ezy_r.at[1], send2.at[5], recv2.at[6], (other, gx, gy_low)),
        remote(ezy_s.at[1], ezy_r.at[0], send2.at[6], recv2.at[5], (other, gx, gy_high)),
        remote(exz_s.at[0], exz_r.at[1], send2.at[7], recv2.at[8], (other, gx_low, gy)),
        remote(exz_s.at[1], exz_r.at[0], send2.at[8], recv2.at[7], (other, gx_high, gy)),
        remote(ys2.at[0, 0], yr2.at[1, 9], send2.at[9], recv2.at[12], (g, gx_low, gy_low)),
        remote(ys2.at[1, 0], yr2.at[0, 9], send2.at[10], recv2.at[11], (g, gx_low, gy_high)),
        remote(ys2.at[0, 7], yr2.at[1, 0], send2.at[11], recv2.at[10], (g, gx_high, gy_low)),
        remote(ys2.at[1, 7], yr2.at[0, 0], send2.at[12], recv2.at[9], (g, gx_high, gy_high)),
    ]
    second[0].start()
    second[1].start()
    z_pack(pred, zs2, PRED_SCALE)
    second[2].start()
    second[3].start()
    second[4].start()
    for side in range(2):
        x = 7 * side
        exz_s[side] = ends(pred, 0, x) * ends(pred, 1, x) * ends(pred, 2, x)
        edge = jnp.zeros((8, 128), jnp.float32)
        for x in range(8):
            here = (lane >= 12 * x) & (lane < 12 * x + 12)
            edge = jnp.where(here, roll_lane(packed_products(ys2[side, x])[1], 12 * x), edge)
        ezy_s[side] = edge
    for copy in second[5:]:
        copy.start()
    gossip_wait(2)
    gossip_send(3)

    second[2].wait_recv()
    z_unpack(pred, zr2, PRED_SCALE)
    for x in range(8):
        for part in (slice(0, 8), slice(56, 64)):
            rho, u0, u1, u2 = (pred[f, x + 2, part, :] for f in range(4))
            m1 = rho * u1
            s01[x + 1, part, :] = m1 * u0
            s11[x, part, :] = m1 * u1
            s12[x, part, :] = m1 * u2
    for i in (3, 4, 5, 6):
        second[i].wait_recv()
    for side in range(2):
        for x in range(8):
            ezy_x[side, x] = roll_lane(ezy_r[side], -12 * x)

    def lighthill(x, carry):
        cross, square = [], []
        for side in range(2):
            along_x = packed_products(yr2[side, x + 2])[0] - packed_products(yr2[side, x])[0]
            _, s12_halo, s22_halo = packed_products(yr2[side, x + 1])
            corner = ezy_x[side, x]
            next_tile = jnp.where(lane >= 10, roll_lane(corner, 10), roll_lane(s12_halo, -2))
            last_tile = jnp.where(lane < 2, roll_lane(corner, -10), roll_lane(s12_halo, 2))
            after = roll_row(jnp.where(row == 0, next_tile, s12_halo), -1)
            before = roll_row(jnp.where(row == 7, last_tile, s12_halo), 1)
            cross.append(along_x + (after - before))
            square.append(s22_halo)
        keep = mask_ref[0, x].astype(jnp.float32)
        for zt in range(ZT):
            part = pl.ds(8 * zt, 8)

            def z(ref, index, dz):
                return ref[index, pl.ds(8 + 8 * zt + dz, 8), :]

            direct = s00[x + 4, part, :] + s00[x, part, :] - 2.0 * s00[x + 2, part, :]
            direct = direct + (z(s11, x, 2) + z(s11, x, -2) - 2.0 * z(s11, x, 0))
            tile = s22[x, part, :]
            ((before, after),) = y_shifts(tile, square[0], square[1], zt, (2,))
            direct = direct + (before + after - 2.0 * tile)
            mixed = (z(s01, x + 2, 1) - z(s01, x + 2, -1)) - (z(s01, x, 1) - z(s01, x, -1))
            tile = (s02[x + 2, part, :] - s02[x, part, :]) + (z(s12, x, 1) - z(s12, x, -1))
            ((before, after),) = y_shifts(tile, cross[0], cross[1], zt, (1,))
            mixed = mixed + (after - before)
            light[pl.ds(pl.multiple_of(x * CZ + 8 * zt, 8), 8), :] = (0.25 * direct + 0.5 * mixed) * keep
        return carry

    lax.fori_loop(2, 6, lighthill, 0)
    second[0].wait_recv()
    second[1].wait_recv()
    x_unpack(pred, xr2, PRED_SCALE)
    for index in (0, 1, 10, 11):
        s00[index] = pred[0, index, 8:56, :] * pred[1, index, 8:56, :] * pred[1, index, 8:56, :]
    for index, layer in ((0, 1), (9, 10)):
        m0 = pred[0, layer, 8:56, :] * pred[1, layer, 8:56, :]
        s01[index, 8:56, :] = m0 * pred[2, layer, 8:56, :]
        s02[index] = m0 * pred[3, layer, 8:56, :]
    for i in range(7, 13):
        second[i].wait_recv()
    for side, index in ((0, 0), (1, 9)):
        s01[index, 0:8, :] = exz_r[side]
        s01[index, 56:64, :] = exz_r[side]
    lax.fori_loop(0, 4, lambda j, carry: lighthill(lax.rem(j + 6, 8), carry), 0)

    pieces = []
    for zp in range(12):
        one, two = (
            light[pl.ds(4 * zp + 2 * i, 8, stride=CZ), :] + light[pl.ds(4 * zp + 2 * i + 1, 8, stride=CZ), :]
            for i in range(2)
        )
        one = one + roll_lane(one, -1)
        two = two + roll_lane(two, 1)
        pieces.append(jnp.where((lane & 1) == 0, one, two))
    merged = jnp.concatenate(pieces, axis=0).astype(jnp.bfloat16)
    source_lane = lax.broadcasted_iota(jnp.int32, (128, 128), 0)
    target_lane = lax.broadcasted_iota(jnp.int32, (128, 128), 1)
    order = jnp.where(target_lane == (source_lane & 1) * 64 + (source_lane >> 1), 1.0, 0.0).astype(jnp.bfloat16)
    sorted_rows = jnp.dot(merged, order, preferred_element_type=jnp.float32)
    tile_rows = jnp.concatenate([sorted_rows[8 * i:8 * i + 8, :] for i in range(12)], axis=1).astype(jnp.bfloat16)
    products = jnp.dot(tile_rows, ops_mat[...], preferred_element_type=jnp.float32)
    pairs = []
    for k in range(4):
        chosen = jnp.zeros((8, 128), jnp.float32)
        for w in range(4):
            chosen = jnp.where(weight_tiles[k] == w, products[:, w * 128:(w + 1) * 128], chosen)
        pairs.append(chosen)
    values = jnp.concatenate(pairs, axis=0)
    high = values.astype(jnp.bfloat16).astype(jnp.float32)
    middle = (values - high).astype(jnp.bfloat16).astype(jnp.float32)
    rest = values - high - middle
    stacked = jnp.concatenate([high, middle, rest, jnp.zeros((32, 128), jnp.float32)], axis=0).astype(jnp.bfloat16)
    sent[...] = jnp.dot(spread[...].astype(jnp.bfloat16), stacked, preferred_element_type=jnp.float32)

    gossip_wait(3)
    all_copies = []
    for d in far_order:
        owner = lax.rem(gx + d, n_gx)
        copy = remote(
            sent.at[pl.ds(pl.multiple_of(owner * 8, 8), 8), :], received.at[gx],
            all_send.at[0], all_recv.at[0], (g, owner, gy),
        )
        copy.start()
    received[gx] = sent[pl.ds(pl.multiple_of(gx * 8, 8), 8), :]

    around = [(dx, dr) for dx in (-1, 0, 1) for dr in (-1, 0, 1) if (dx, dr) != (0, 0)]

    def neighbour(dx, dr):
        there = lax.rem(rank + (n_rank + dr), n_rank)
        return (there // n_gy, lax.rem(gx + (n_gx + dx), n_gx), lax.rem(there, n_gy))

    def slot_of(dx, dr):
        return around.index((dx, dr))

    for dx, dr in around:
        remote(
            wave_ref, near_wave.at[slot_of(-dx, -dr)], wave_send.at[0], wave_recv.at[0], neighbour(dx, dr)
        ).start()

    def second_rate(x, carry):
        low, high = yr2[0, x + 1], yr2[1, x + 1]
        for zt in range(ZT):
            _, rates = rate_tile(pred, x, zt, low, high)
            part = pl.ds(8 * zt, 8)
            for f in range(5):
                base_sum[f, x, part, :] = base_sum[f, x, part, :] + (0.5 * LES_STEP) * rates[f]
        return carry

    lax.fori_loop(0, CX, second_rate, 0)
    store_les = pltpu.make_async_copy(base_sum, les_out, local_sems.at[2])
    store_les.start()

    others = received.at[0:n_gx - 1]
    pltpu.make_async_copy(others, others, all_recv.at[0]).wait()
    own_source[...] = jnp.sum(received[...], axis=0)
    for dx, dr in around:
        remote(
            own_source, near_source.at[slot_of(-dx, -dr)], src_send.at[0], src_recv.at[0], neighbour(dx, dr)
        ).start()

    pltpu.make_async_copy(near_wave, near_wave, wave_recv.at[0]).wait()
    wide_row = lax.broadcasted_iota(jnp.int32, (24, 256), 0)
    wide_lane = lax.broadcasted_iota(jnp.int32, (24, 256), 1)

    def flag(yes):
        return yes.astype(jnp.int32).astype(jnp.float32)

    inside = jnp.where(wide_row < 8, flag(gx > 0), jnp.where(wide_row >= 16, flag(gx < n_gx - 1), 1.0))
    inside = inside * jnp.where(
        wide_lane < 128, 1.0, jnp.where(wide_lane < 192, flag(rank < n_rank - 1), flag(rank > 0))
    )
    column = jnp.where(wide_lane < 192, wide_lane, wide_lane - 256) + rank * 128
    inverse_radius = 1.0 / (column.astype(jnp.float32) + 0.5)

    def assemble(block):
        strips = []
        for dx in (-1, 0, 1):
            side = jnp.where(lane < 64, block(dx, 1), block(dx, -1))
            strips.append(jnp.concatenate([block(dx, 0), side], axis=1))
        return jnp.concatenate(strips, axis=0) * inside

    def wave_block(f):
        return lambda dx, dr: wave_ref[f] if (dx, dr) == (0, 0) else near_wave[slot_of(dx, dr), f]

    now = [assemble(wave_block(f)) for f in range(3)]
    pltpu.make_async_copy(near_source, near_source, src_recv.at[0]).wait()
    source = assemble(lambda dx, dr: own_source[...] if (dx, dr) == (0, 0) else near_source[slot_of(dx, dr)])
    for _ in range(2):
        rate_one = wave_rates(now, source, inverse_radius)
        ahead = [(v + WAVE_STEP * r) * inside for v, r in zip(now, rate_one)]
        rate_two = wave_rates(ahead, source, inverse_radius)
        now = [(v + (0.5 * WAVE_STEP) * (a + b)) * inside for v, a, b in zip(now, rate_one, rate_two)]
    for f in range(3):
        wave_out[f] = now[f][8:16, 0:128]

    for copy in first + second:
        copy.wait_send()
    pltpu.make_async_copy(others, others, all_send.at[0]).wait()
    pltpu.make_async_copy(near_wave, near_wave, wave_send.at[0]).wait()
    pltpu.make_async_copy(near_source, near_source, src_send.at[0]).wait()
    store_les.wait()


def on_device(sizes, les_state, wave_state, restriction_ops, pair_owner, pair_slot, pair_weight, tile_mask):
    n_gx = sizes[1]
    tile_len, op_count, width = restriction_ops.shape
    ops_flat = restriction_ops.reshape(tile_len * op_count, width)
    rounds = max(1, (n_gx // 2).bit_length() - 1)
    far_order = sorted(range(1, n_gx), key=lambda d: -(2 * min(d // 8, 4 - d // 8) + min(d % 8, 8 - d % 8)))
    f32, i32, bf16 = jnp.float32, jnp.int32, jnp.bfloat16
    vmem, dma = pltpu.VMEM, pltpu.SemaphoreType.DMA
    scratch = [
        vmem((5, 12, 64, 128), f32), vmem((5, 12, 64, 128), f32), vmem((5, 8, 48, 128), f32),
        vmem((12, 48, 128), f32), vmem((8, 64, 128), f32), vmem((8, 48, 128), f32),
        vmem((10, 64, 128), f32), vmem((10, 48, 128), f32), vmem((8, 64, 128), f32),
        vmem((2, 5, 48, 128), i32), vmem((2, 5, 48, 128), i32), vmem((2, 5, 48, 128), i32), vmem((2, 5, 48, 128), i32),
        vmem((10, 8, 128), i32), vmem((10, 8, 128), i32), vmem((10, 8, 128), i32), vmem((10, 8, 128), i32),
        vmem((2, 8, 8, 128), f32), vmem((2, 8, 8, 128), f32), vmem((2, 8, 8, 128), f32), vmem((2, 10, 8, 128), f32),
        vmem((2, 8, 128), f32), vmem((2, 8, 128), f32), vmem((2, 8, 128), f32), vmem((2, 8, 128), f32),
        vmem((2, 8, 8, 128), f32),
        vmem((CX * CZ, 128), f32), vmem((6144, 128), bf16), vmem((512, 128), f32), vmem((1536, 512), bf16),
        vmem((n_gx * 8, 128), f32), vmem((4, 8, 128), i32),
        vmem((n_gx * 8, 128), f32), vmem((n_gx, 8, 128), f32), vmem((8, 128), f32),
        vmem((8, 8, 128), f32), vmem((8, 3, 8, 128), f32),
        dma((3,)), dma((5,)), dma((5,)), dma((13,)), dma((13,)), dma((1,)), dma((1,)), dma((1,)), dma((1,)),
        dma((1,)), dma((1,)), pltpu.SemaphoreType.REGULAR((rounds,)),
    ]
    any_space = pl.BlockSpec(memory_space=pl.ANY)
    in_vmem = pl.BlockSpec(memory_space=pltpu.VMEM)
    in_smem = pl.BlockSpec(memory_space=pltpu.SMEM)
    return pl.pallas_call(
        functools.partial(kernel, sizes, far_order),
        out_shape=(
            jax.ShapeDtypeStruct(les_state.shape, f32),
            jax.ShapeDtypeStruct(wave_state.shape, f32),
        ),
        in_specs=[any_space, in_vmem, any_space, in_smem, in_smem, in_smem, in_smem],
        out_specs=(any_space, in_vmem),
        scratch_shapes=scratch,
        compiler_params=pltpu.CompilerParams(collective_id=0, has_side_effects=True),
        name="jet_step",
    )(les_state, wave_state, ops_flat, *(a.swapaxes(1, 2) for a in (pair_owner, pair_slot, pair_weight)), tile_mask)


def solution(mesh):
    sizes = (mesh.shape["group"], mesh.shape["gx"], mesh.shape["gy"])
    return jax.shard_map(
        functools.partial(on_device, sizes),
        mesh=mesh,
        in_specs=(
            P(None, "gx", "group", "gy"),
            P(None, "gx", ("group", "gy")),
            P(),
            P(("group", "gy"), "gx", None),
            P(("group", "gy"), "gx", None),
            P(("group", "gy"), "gx", None),
            P(("group", "gy"), "gx"),
        ),
        out_specs=(P(None, "gx", "group", "gy"), P(None, "gx", ("group", "gy"))),
        check_vma=False,
    )
```

time: 253 us -> 57 us (0.23)
  the two profiles are of different devices: /device:TPU:39 before, /device:TPU:1 now
where the time goes in v1:
time: 57 us; the launch traced here: 56.8 us
  Pallas kernels  53.3 us (94%)
  local copies, waits for them, and re-layouts  2.85 us (5%)
  between operations  0.65 us (1%)
    pallas_call x1, Pallas kernels, on_device(): pl.pallas_call(functools.partial(kernel, sizes, far_order), out_shape=(ja...  53.3 us
    unnamed x4, local copies, waits for them, and re-layouts  2.85 us

profile of v1, /device:TPU:1, one launch (start us, length us, event | category | flops | bytes accessed | tf_op | source)
XLA Modules:
  0.0 56.8 jit_solution(3773426882719520252)
XLA Ops:
  0.6 53.3 %jet_step.1 = (f32[5,8,48,128]{3,2,1,0:T(8,128)}, f32[3,8,128]{2,1,0:T(8,128)}) custom-call(f32[5,8,48,128]{3,2,1,0:T(8,128)} %les_ref.1, f32[3,8,128]{2,1,0:T(8,128)} %wave_ref.1, bf16[6144,128]{1,0:T(8,128)(2,1)} %bitcast.4, s32[1,4,8]{2,1,0:T(4,128)} %bitcast.5, s32[1,4,8]{2,1,0:T(4,128)} %bitcast.6, s32[1,4,8]{2,1,0:T(4,128)} %bitcast.7, s32[1,8]{1,0:T(1,128)} %mask_ref.1), custom_call_target="tpu_custom_call" | custom-call | tf_op jit(solution)/shard_map/jet_step/pallas_call | solution.py:539
  53.9 0.0 copy-start
  53.9 2.2 %copy.11 = f32[5,8,48,128]{3,2,1,0:T(8,128)} copy(f32[5,8,48,128]{3,2,1,0:T(8,128)} %get-tuple-element.4) | data formatting | bytes 1966080
  56.2 0.0 copy-done
  56.2 0.6 %copy.12 = f32[3,8,128]{2,1,0:T(8,128)} copy(f32[3,8,128]{2,1,0:T(8,128)S(1)} %copy-done) | data formatting | bytes 24576
Async XLA Ops:
  53.9 2.3 %copy-start = (f32[3,8,128]{2,1,0:T(8,128)S(1)}, f32[3,8,128]{2,1,0:T(8,128)}, u32[]{:S(2)}) copy-start(f32[3,8,128]{2,1,0:T(8,128)} %get-tuple-element.5) | copy-start | bytes 36868

commit v2 on v1

--- a/solution.py
+++ b/solution.py
@@ -53,18 +53,18 @@
     return pltpu.roll(tile, shift, 0) if shift else tile
 
 
-def y_shifts(tile, low, high, slot, reach):
+def y_shifts(tile, halo, slot, reach):
     lane = lanes()
-    low, high = roll_lane(low, 126 - 2 * slot), roll_lane(high, -2 * slot)
+    halo = roll_lane(halo, -(4 * slot + 2))
     shifts = []
     for s in reach:
-        before = roll_lane(jnp.where(lane >= 128 - s, low, tile), s)
-        after = roll_lane(jnp.where(lane < s, high, tile), -s)
+        before = roll_lane(jnp.where(lane >= 128 - s, halo, tile), s)
+        after = roll_lane(jnp.where(lane < s, halo, tile), -s)
         shifts.append((before, after))
     return shifts
 
 
-def rate_tile(buf, x, zt, low, high):
+def rate_tile(buf, x, zt, halo):
     base = 8 + 8 * zt
 
     def at(f, dx, dz):
@@ -74,7 +74,7 @@
     for f in range(5):
         c = at(f, 0, 0)
         xm1, xp1, zm1, zp1 = at(f, -1, 0), at(f, 1, 0), at(f, 0, -1), at(f, 0, 1)
-        (ym1, yp1), (ym2, yp2) = y_shifts(c, low, high, f * ZT + zt, (1, 2))
+        (ym1, yp1), (ym2, yp2) = y_shifts(c, halo, f * ZT + zt, (1, 2))
         dx = 8.0 * (xp1 - xm1) - (at(f, 2, 0) - at(f, -2, 0))
         dz = 8.0 * (zp1 - zm1) - (at(f, 0, 2) - at(f, 0, -2))
         dy = 8.0 * (yp1 - ym1) - (yp2 - ym2)
@@ -97,11 +97,11 @@
 
 
 def packed_products(tile):
-    momentum = tile * roll_lane(tile, -36)
+    momentum = tile * roll_lane(tile, -72)
     return (
-        momentum * roll_lane(tile, -12),
         momentum * roll_lane(tile, -24),
-        momentum * roll_lane(tile, -36),
+        momentum * roll_lane(tile, -48),
+        momentum * roll_lane(tile, -72),
     )
 
 
@@ -119,14 +119,15 @@
 
 def kernel(
     sizes, far_order,
-    les_ref, wave_ref, ops_ref, owner_ref, slot_ref, weight_ref, mask_ref,
+    les_ref, wave_in, ops_ref, owner_in, slot_in, weight_in, mask_in,
     les_out, wave_out,
     state, pred, base_sum, s00, s11, s22, s01, s02, s12,
-    xs1, xr1, xs2, xr2, zs1, zr1, zs2, zr2, ys1, yr1, ys2, yr2,
+    wave_ref, owner_ref, slot_ref, weight_ref, mask_ref,
+    xs1, xr1, xs2, xr2, zs1, zr1, zs2, zr2, ys1, yr1, ys2, yr2, ym2,
     exz_s, exz_r, ezy_s, ezy_r, ezy_x,
     light, ops_raw, ops_wide, ops_mat, spread, weight_tiles,
     sent, received, own_source, near_source, near_wave,
-    local_sems, send1, recv1, send2, recv2, wave_send, wave_recv, all_send, all_recv, src_send, src_recv, gossip,
+    local_sems, x_send, x_recv, send1, recv1, send2, recv2, wave_send, wave_recv, all_send, all_recv, src_send, src_recv, gossip,
 ):
     n_group, n_gx, n_gy = sizes
     g, gx, gy = lax.axis_index("group"), lax.axis_index("gx"), lax.axis_index("gy")
@@ -146,11 +147,26 @@
     for device in ((g, gx_low, gy), (g, gx_high, gy), (other, gx, gy), (g, gx, gy_low), (g, gx, gy_high)):
         pl.semaphore_signal(barrier, inc=1, device_id=device, device_id_type=MESH)
 
-    load_les = pltpu.make_async_copy(les_ref, state.at[:, 2:10, 8:56, :], local_sems.at[0])
-    load_les.start()
-    load_ops = pltpu.make_async_copy(ops_ref, ops_raw, local_sems.at[1])
-    load_ops.start()
-    load_les.wait()
+    def load(src, dst, i):
+        copy = pltpu.make_async_copy(src, dst, local_sems.at[i])
+        copy.start()
+        return copy
+
+    load_faces = [
+        load(les_ref.at[:, 0:2], state.at[:, 2:4, 8:56, :], 0),
+        load(les_ref.at[:, 6:8], state.at[:, 8:10, 8:56, :], 1),
+    ]
+    load_inner = load(les_ref.at[:, 2:6], state.at[:, 4:8, 8:56, :], 2)
+    load_small = [
+        load(owner_in, owner_ref, 3),
+        load(slot_in, slot_ref, 4),
+        load(weight_in, weight_ref, 5),
+        load(mask_in, mask_ref, 6),
+        load(wave_in, wave_ref, 7),
+    ]
+    load_ops = load(ops_ref, ops_raw, 8)
+    for copy in load_faces:
+        copy.wait()
 
     def gossip_send(r):
         if r < gossip.shape[0]:
@@ -162,19 +178,32 @@
         if r < gossip.shape[0]:
             pl.semaphore_wait(gossip.at[r], 2)
 
-    def x_pack(buf, out, scales, layer):
+    def x_pack(buf, out, scales, chunk):
+        part = slice(8 + 24 * chunk, 32 + 24 * chunk)
         for f in range(5):
             for side, first in ((0, 2), (1, 8)):
-                out[side, f] = pair_words(
-                    buf[f, first, 8:56, :], buf[f, first + 1, 8:56, :], OFFSETS[f], scales[f]
+                out[side, chunk, f] = pair_words(
+                    buf[f, first, part, :], buf[f, first + 1, part, :], OFFSETS[f], scales[f]
                 )
 
-    def x_unpack(buf, words, scales):
+    def x_unpack(buf, words, scales, chunk):
+        part = slice(8 + 24 * chunk, 32 + 24 * chunk)
         for f in range(5):
             for side, first in ((0, 0), (1, 10)):
-                one, two = split_words(words[side, f], OFFSETS[f], scales[f])
-                buf[f, first, 8:56, :] = one
-                buf[f, first + 1, 8:56, :] = two
+                one, two = split_words(words[side, chunk, f], OFFSETS[f], scales[f])
+                buf[f, first, part, :] = one
+                buf[f, first + 1, part, :] = two
+
+    def x_copies(sent_words, words, stage, chunk):
+        first = 4 * stage + 2 * chunk
+        return [
+            remote(
+                sent_words.at[0, chunk], words.at[1, chunk], x_send.at[first], x_recv.at[first + 1], (g, gx_low, gy)
+            ),
+            remote(
+                sent_words.at[1, chunk], words.at[0, chunk], x_send.at[first + 1], x_recv.at[first], (g, gx_high, gy)
+            ),
+        ]
 
     def ends(buf, f, x):
         return jnp.where(row < 4, buf[f, x + 2, 8:16, :], buf[f, x + 2, 48:56, :])
@@ -196,40 +225,44 @@
                         buf[f, x + 2, 56:64, :] = tile
 
     def y_add(packed, tile, slot):
-        here = (lane >> 1) == slot
-        return (
-            jnp.where(here, roll_lane(tile, 2 * slot), packed[0]),
-            jnp.where(here, roll_lane(tile, 2 * slot + 2), packed[1]),
-        )
+        return jnp.where((lane >> 2) == slot, roll_lane(tile, 4 * slot + 2), packed)
+
+    def y_merge(from_low, from_high):
+        return jnp.where((lane & 2) == 0, from_low, from_high)
 
     def y_pack(x, carry):
-        packed = (jnp.zeros((8, 128), jnp.float32),) * 2
+        packed = jnp.zeros((8, 128), jnp.float32)
         for f in range(5):
             for zt in range(ZT):
                 packed = y_add(packed, state[f, x + 2, pl.ds(8 + 8 * zt, 8), :], f * ZT + zt)
-        ys1[0, x] = packed[0]
-        ys1[1, x] = packed[1]
+        ys1[x] = packed
         return carry
 
     x_pack(state, xs1, STATE_SCALE, 0)
     pl.semaphore_wait(barrier, 5)
     gossip_send(0)
+    x_first = [x_copies(xs1, xr1, 0, chunk) for chunk in range(2)]
+    x_second = [x_copies(xs2, xr2, 1, chunk) for chunk in range(2)]
     first = [
-        remote(xs1.at[0], xr1.at[1], send1.at[0], recv1.at[1], (g, gx_low, gy)),
-        remote(xs1.at[1], xr1.at[0], send1.at[1], recv1.at[0], (g, gx_high, gy)),
-        remote(zs1, zr1, send1.at[2], recv1.at[2], (other, gx, gy)),
-        remote(ys1.at[0], yr1.at[1], send1.at[3], recv1.at[4], (g, gx, gy_low)),
-        remote(ys1.at[1], yr1.at[0], send1.at[4], recv1.at[3], (g, gx, gy_high)),
+        remote(zs1, zr1, send1.at[0], recv1.at[0], (other, gx, gy)),
+        remote(ys1, yr1.at[1], send1.at[1], recv1.at[2], (g, gx, gy_low)),
+        remote(ys1, yr1.at[0], send1.at[2], recv1.at[1], (g, gx, gy_high)),
     ]
+    for copy in x_first[0]:
+        copy.start()
+    x_pack(state, xs1, STATE_SCALE, 1)
+    for copy in x_first[1]:
+        copy.start()
+    load_inner.wait()
+    z_pack(state, zs1, STATE_SCALE)
     first[0].start()
+    lax.fori_loop(0, CX, y_pack, 0)
     first[1].start()
-    z_pack(state, zs1, STATE_SCALE)
     first[2].start()
-    lax.fori_loop(0, CX, y_pack, 0)
-    first[3].start()
-    first[4].start()
 
     load_ops.wait()
+    for copy in load_small:
+        copy.wait()
 
     def widen(i, carry):
         part = pl.ds(pl.multiple_of(i * 512, 512), 512)
@@ -254,16 +287,16 @@
 
     gossip_wait(0)
     gossip_send(1)
+    first[0].wait_recv()
+    z_unpack(state, zr1, STATE_SCALE)
+    first[1].wait_recv()
     first[2].wait_recv()
-    z_unpack(state, zr1, STATE_SCALE)
-    first[3].wait_recv()
-    first[4].wait_recv()
-
-    def first_rate(x, carry):
-        low, high = yr1[0, x], yr1[1, x]
-        packed = (jnp.zeros((8, 128), jnp.float32),) * 2
-        for zt in range(ZT):
-            centre, rates = rate_tile(state, x, zt, low, high)
+
+    def first_rate(x, tiles):
+        halo = y_merge(yr1[0, x], yr1[1, x])
+        packed = jnp.zeros((8, 128), jnp.float32) if tiles[0] == 0 else ys2[x]
+        for zt in tiles:
+            centre, rates = rate_tile(state, x, zt, halo)
             part = pl.ds(8 * zt, 8)
             inner = pl.ds(8 + 8 * zt, 8)
             new = []
@@ -281,54 +314,62 @@
             s11[x, inner, :] = m1 * u1
             s12[x, inner, :] = m1 * u2
             s22[x, part, :] = rho * u2 * u2
-        ys2[0, x] = packed[0]
-        ys2[1, x] = packed[1]
+        ys2[x] = packed
+
+    def rate_inner(x, carry):
+        first_rate(x, tuple(range(ZT)))
         return carry
 
-    lax.fori_loop(2, 6, first_rate, 0)
+    lax.fori_loop(2, 6, rate_inner, 0)
     gossip_wait(1)
     gossip_send(2)
-    first[0].wait_recv()
-    first[1].wait_recv()
-    x_unpack(state, xr1, STATE_SCALE)
-    lax.fori_loop(0, 4, lambda j, carry: first_rate(lax.rem(j + 6, 8), carry), 0)
-
-    x_pack(pred, xs2, PRED_SCALE, 0)
+    for chunk in range(2):
+        for copy in x_first[chunk]:
+            copy.wait_recv()
+        x_unpack(state, xr1, STATE_SCALE, chunk)
+
+        def rate_outer(j, carry):
+            first_rate(lax.rem(j + 6, 8), tuple(range(3 * chunk, 3 * chunk + 3)))
+            return carry
+
+        lax.fori_loop(0, 4, rate_outer, 0)
+        x_pack(pred, xs2, PRED_SCALE, chunk)
+        for copy in x_second[chunk]:
+            copy.start()
+
     second = [
-        remote(xs2.at[0], xr2.at[1], send2.at[0], recv2.at[1], (g, gx_low, gy)),
-        remote(xs2.at[1], xr2.at[0], send2.at[1], recv2.at[0], (g, gx_high, gy)),
-        remote(zs2, zr2, send2.at[2], recv2.at[2], (other, gx, gy)),
-        remote(ys2.at[0], yr2.at[1, 1:9], send2.at[3], recv2.at[4], (g, gx, gy_low)),
-        remote(ys2.at[1], yr2.at[0, 1:9], send2.at[4], recv2.at[3], (g, gx, gy_high)),
-        remote(ezy_s.at[0], ezy_r.at[1], send2.at[5], recv2.at[6], (other, gx, gy_low)),
-        remote(ezy_s.at[1], ezy_r.at[0], send2.at[6], recv2.at[5], (other, gx, gy_high)),
-        remote(exz_s.at[0], exz_r.at[1], send2.at[7], recv2.at[8], (other, gx_low, gy)),
-        remote(exz_s.at[1], exz_r.at[0], send2.at[8], recv2.at[7], (other, gx_high, gy)),
-        remote(ys2.at[0, 0], yr2.at[1, 9], send2.at[9], recv2.at[12], (g, gx_low, gy_low)),
-        remote(ys2.at[1, 0], yr2.at[0, 9], send2.at[10], recv2.at[11], (g, gx_low, gy_high)),
-        remote(ys2.at[0, 7], yr2.at[1, 0], send2.at[11], recv2.at[10], (g, gx_high, gy_low)),
-        remote(ys2.at[1, 7], yr2.at[0, 0], send2.at[12], recv2.at[9], (g, gx_high, gy_high)),
+        remote(zs2, zr2, send2.at[0], recv2.at[0], (other, gx, gy)),
+        remote(ys2, yr2.at[1, 1:9], send2.at[1], recv2.at[2], (g, gx, gy_low)),
+        remote(ys2, yr2.at[0, 1:9], send2.at[2], recv2.at[1], (g, gx, gy_high)),
+        remote(ezy_s, ezy_r.at[1], send2.at[3], recv2.at[4], (other, gx, gy_low)),
+        remote(ezy_s, ezy_r.at[0], send2.at[4], recv2.at[3], (other, gx, gy_high)),
+        remote(exz_s.at[0], exz_r.at[1], send2.at[5], recv2.at[6], (other, gx_low, gy)),
+        remote(exz_s.at[1], exz_r.at[0], send2.at[6], recv2.at[5], (other, gx_high, gy)),
+        remote(ys2.at[0], yr2.at[1, 9], send2.at[7], recv2.at[10], (g, gx_low, gy_low)),
+        remote(ys2.at[0], yr2.at[0, 9], send2.at[8], recv2.at[9], (g, gx_low, gy_high)),
+        remote(ys2.at[7], yr2.at[1, 0], send2.at[9], recv2.at[8], (g, gx_high, gy_low)),
+        remote(ys2.at[7], yr2.at[0, 0], send2.at[10], recv2.at[7], (g, gx_high, gy_high)),
     ]
-    second[0].start()
-    second[1].start()
-    z_pack(pred, zs2, PRED_SCALE)
-    second[2].start()
-    second[3].start()
-    second[4].start()
     for side in range(2):
         x = 7 * side
         exz_s[side] = ends(pred, 0, x) * ends(pred, 1, x) * ends(pred, 2, x)
-        edge = jnp.zeros((8, 128), jnp.float32)
-        for x in range(8):
-            here = (lane >= 12 * x) & (lane < 12 * x + 12)
-            edge = jnp.where(here, roll_lane(packed_products(ys2[side, x])[1], 12 * x), edge)
-        ezy_s[side] = edge
     for copy in second[5:]:
         copy.start()
+    z_pack(pred, zs2, PRED_SCALE)
+    for copy in second[:3]:
+        copy.start()
+    edge = jnp.zeros((8, 128), jnp.float32)
+    for x in range(8):
+        product = packed_products(ys2[x])[1]
+        both = jnp.where(lane < 4, product, roll_lane(product, -16))
+        edge = jnp.where((lane >> 3) == x, roll_lane(both, 8 * x), edge)
+    ezy_s[...] = edge
+    second[3].start()
+    second[4].start()
     gossip_wait(2)
     gossip_send(3)
 
-    second[2].wait_recv()
+    second[0].wait_recv()
     z_unpack(pred, zr2, PRED_SCALE)
     for x in range(8):
         for part in (slice(0, 8), slice(56, 64)):
@@ -337,24 +378,23 @@
             s01[x + 1, part, :] = m1 * u0
             s11[x, part, :] = m1 * u1
             s12[x, part, :] = m1 * u2
-    for i in (3, 4, 5, 6):
-        second[i].wait_recv()
-    for side in range(2):
-        for x in range(8):
-            ezy_x[side, x] = roll_lane(ezy_r[side], -12 * x)
+    for copy in second[1:5]:
+        copy.wait_recv()
+    for x in range(8):
+        ym2[x + 1] = y_merge(yr2[0, x + 1], yr2[1, x + 1])
+    corners = y_merge(ezy_r[0], ezy_r[1])
+    for x in range(8):
+        ezy_x[x] = roll_lane(corners, -8 * x)
 
     def lighthill(x, carry):
-        cross, square = [], []
-        for side in range(2):
-            along_x = packed_products(yr2[side, x + 2])[0] - packed_products(yr2[side, x])[0]
-            _, s12_halo, s22_halo = packed_products(yr2[side, x + 1])
-            corner = ezy_x[side, x]
-            next_tile = jnp.where(lane >= 10, roll_lane(corner, 10), roll_lane(s12_halo, -2))
-            last_tile = jnp.where(lane < 2, roll_lane(corner, -10), roll_lane(s12_halo, 2))
-            after = roll_row(jnp.where(row == 0, next_tile, s12_halo), -1)
-            before = roll_row(jnp.where(row == 7, last_tile, s12_halo), 1)
-            cross.append(along_x + (after - before))
-            square.append(s22_halo)
+        along_x = packed_products(ym2[x + 2])[0] - packed_products(ym2[x])[0]
+        _, s12_halo, square = packed_products(ym2[x + 1])
+        corner = ezy_x[x]
+        next_tile = jnp.where(lane >= 20, roll_lane(corner, 20), roll_lane(s12_halo, -4))
+        last_tile = jnp.where(lane < 4, roll_lane(corner, -4), roll_lane(s12_halo, 4))
+        after = roll_row(jnp.where(row == 0, next_tile, s12_halo), -1)
+        before = roll_row(jnp.where(row == 7, last_tile, s12_halo), 1)
+        cross = along_x + (after - before)
         keep = mask_ref[0, x].astype(jnp.float32)
         for zt in range(ZT):
             part = pl.ds(8 * zt, 8)
@@ -365,27 +405,30 @@
             direct = s00[x + 4, part, :] + s00[x, part, :] - 2.0 * s00[x + 2, part, :]
             direct = direct + (z(s11, x, 2) + z(s11, x, -2) - 2.0 * z(s11, x, 0))
             tile = s22[x, part, :]
-            ((before, after),) = y_shifts(tile, square[0], square[1], zt, (2,))
+            ((before, after),) = y_shifts(tile, square, zt, (2,))
             direct = direct + (before + after - 2.0 * tile)
             mixed = (z(s01, x + 2, 1) - z(s01, x + 2, -1)) - (z(s01, x, 1) - z(s01, x, -1))
             tile = (s02[x + 2, part, :] - s02[x, part, :]) + (z(s12, x, 1) - z(s12, x, -1))
-            ((before, after),) = y_shifts(tile, cross[0], cross[1], zt, (1,))
+            ((before, after),) = y_shifts(tile, cross, zt, (1,))
             mixed = mixed + (after - before)
             light[pl.ds(pl.multiple_of(x * CZ + 8 * zt, 8), 8), :] = (0.25 * direct + 0.5 * mixed) * keep
         return carry
 
     lax.fori_loop(2, 6, lighthill, 0)
-    second[0].wait_recv()
-    second[1].wait_recv()
-    x_unpack(pred, xr2, PRED_SCALE)
+    for chunk in range(2):
+        for copy in x_second[chunk]:
+            copy.wait_recv()
+        x_unpack(pred, xr2, PRED_SCALE, chunk)
     for index in (0, 1, 10, 11):
         s00[index] = pred[0, index, 8:56, :] * pred[1, index, 8:56, :] * pred[1, index, 8:56, :]
     for index, layer in ((0, 1), (9, 10)):
         m0 = pred[0, layer, 8:56, :] * pred[1, layer, 8:56, :]
         s01[index, 8:56, :] = m0 * pred[2, layer, 8:56, :]
         s02[index] = m0 * pred[3, layer, 8:56, :]
-    for i in range(7, 13):
-        second[i].wait_recv()
+    for copy in second[5:]:
+        copy.wait_recv()
+    for index in (0, 9):
+        ym2[index] = y_merge(yr2[0, index], yr2[1, index])
     for side, index in ((0, 0), (1, 9)):
         s01[index, 0:8, :] = exz_r[side]
         s01[index, 56:64, :] = exz_r[side]
@@ -446,16 +489,16 @@
         ).start()
 
     def second_rate(x, carry):
-        low, high = yr2[0, x + 1], yr2[1, x + 1]
+        halo = ym2[x + 1]
         for zt in range(ZT):
-            _, rates = rate_tile(pred, x, zt, low, high)
+            _, rates = rate_tile(pred, x, zt, halo)
             part = pl.ds(8 * zt, 8)
             for f in range(5):
                 base_sum[f, x, part, :] = base_sum[f, x, part, :] + (0.5 * LES_STEP) * rates[f]
         return carry
 
     lax.fori_loop(0, CX, second_rate, 0)
-    store_les = pltpu.make_async_copy(base_sum, les_out, local_sems.at[2])
+    store_les = pltpu.make_async_copy(base_sum, les_out, local_sems.at[0])
     store_les.start()
 
     others = received.at[0:n_gx - 1]
@@ -501,12 +544,25 @@
     for f in range(3):
         wave_out[f] = now[f][8:16, 0:128]
 
-    for copy in first + second:
+    for copy in first + second + x_first[0] + x_first[1] + x_second[0] + x_second[1]:
         copy.wait_send()
     pltpu.make_async_copy(others, others, all_send.at[0]).wait()
     pltpu.make_async_copy(near_wave, near_wave, wave_send.at[0]).wait()
     pltpu.make_async_copy(near_source, near_source, src_send.at[0]).wait()
     store_les.wait()
+
+
+def hand_on(les_in, wave_in, les_out, wave_out, les_buf, wave_buf, in_sems, out_sems):
+    legs = [(wave_in, wave_buf, wave_out)] + [(les_in.at[f], les_buf.at[f], les_out.at[f]) for f in range(5)]
+    into = [pltpu.make_async_copy(a, b, in_sems.at[i]) for i, (a, b, _) in enumerate(legs)]
+    out = [pltpu.make_async_copy(b, c, out_sems.at[i]) for i, (_, b, c) in enumerate(legs)]
+    for copy in into:
+        copy.start()
+    for one, two in zip(into, out):
+        one.wait()
+        two.start()
+    for copy in out:
+        copy.wait()
 
 
 def on_device(sizes, les_state, wave_state, restriction_ops, pair_owner, pair_slot, pair_weight, tile_mask):
@@ -516,38 +572,48 @@
     rounds = max(1, (n_gx // 2).bit_length() - 1)
     far_order = sorted(range(1, n_gx), key=lambda d: -(2 * min(d // 8, 4 - d // 8) + min(d % 8, 8 - d % 8)))
     f32, i32, bf16 = jnp.float32, jnp.int32, jnp.bfloat16
-    vmem, dma = pltpu.VMEM, pltpu.SemaphoreType.DMA
+    vmem, smem, dma = pltpu.VMEM, pltpu.SMEM, pltpu.SemaphoreType.DMA
     scratch = [
         vmem((5, 12, 64, 128), f32), vmem((5, 12, 64, 128), f32), vmem((5, 8, 48, 128), f32),
         vmem((12, 48, 128), f32), vmem((8, 64, 128), f32), vmem((8, 48, 128), f32),
         vmem((10, 64, 128), f32), vmem((10, 48, 128), f32), vmem((8, 64, 128), f32),
-        vmem((2, 5, 48, 128), i32), vmem((2, 5, 48, 128), i32), vmem((2, 5, 48, 128), i32), vmem((2, 5, 48, 128), i32),
+        vmem((3, 8, 128), f32), smem((1, 4, 8), i32), smem((1, 4, 8), i32), smem((1, 4, 8), i32), smem((1, 8), i32),
+        vmem((2, 2, 5, 24, 128), i32), vmem((2, 2, 5, 24, 128), i32),
+        vmem((2, 2, 5, 24, 128), i32), vmem((2, 2, 5, 24, 128), i32),
         vmem((10, 8, 128), i32), vmem((10, 8, 128), i32), vmem((10, 8, 128), i32), vmem((10, 8, 128), i32),
-        vmem((2, 8, 8, 128), f32), vmem((2, 8, 8, 128), f32), vmem((2, 8, 8, 128), f32), vmem((2, 10, 8, 128), f32),
-        vmem((2, 8, 128), f32), vmem((2, 8, 128), f32), vmem((2, 8, 128), f32), vmem((2, 8, 128), f32),
-        vmem((2, 8, 8, 128), f32),
+        vmem((8, 8, 128), f32), vmem((2, 8, 8, 128), f32), vmem((8, 8, 128), f32), vmem((2, 10, 8, 128), f32),
+        vmem((10, 8, 128), f32),
+        vmem((2, 8, 128), f32), vmem((2, 8, 128), f32), vmem((8, 128), f32), vmem((2, 8, 128), f32),
+        vmem((8, 8, 128), f32),
         vmem((CX * CZ, 128), f32), vmem((6144, 128), bf16), vmem((512, 128), f32), vmem((1536, 512), bf16),
         vmem((n_gx * 8, 128), f32), vmem((4, 8, 128), i32),
         vmem((n_gx * 8, 128), f32), vmem((n_gx, 8, 128), f32), vmem((8, 128), f32),
         vmem((8, 8, 128), f32), vmem((8, 3, 8, 128), f32),
-        dma((3,)), dma((5,)), dma((5,)), dma((13,)), dma((13,)), dma((1,)), dma((1,)), dma((1,)), dma((1,)),
+        dma((9,)), dma((8,)), dma((8,)), dma((3,)), dma((3,)), dma((11,)), dma((11,)), dma((1,)), dma((1,)), dma((1,)), dma((1,)),
         dma((1,)), dma((1,)), pltpu.SemaphoreType.REGULAR((rounds,)),
     ]
     any_space = pl.BlockSpec(memory_space=pl.ANY)
     in_vmem = pl.BlockSpec(memory_space=pltpu.VMEM)
-    in_smem = pl.BlockSpec(memory_space=pltpu.SMEM)
-    return pl.pallas_call(
+    results = pl.pallas_call(
         functools.partial(kernel, sizes, far_order),
         out_shape=(
             jax.ShapeDtypeStruct(les_state.shape, f32),
             jax.ShapeDtypeStruct(wave_state.shape, f32),
         ),
-        in_specs=[any_space, in_vmem, any_space, in_smem, in_smem, in_smem, in_smem],
+        in_specs=[any_space] * 7,
         out_specs=(any_space, in_vmem),
         scratch_shapes=scratch,
         compiler_params=pltpu.CompilerParams(collective_id=0, has_side_effects=True),
         name="jet_step",
     )(les_state, wave_state, ops_flat, *(a.swapaxes(1, 2) for a in (pair_owner, pair_slot, pair_weight)), tile_mask)
+    return pl.pallas_call(
+        hand_on,
+        out_shape=tuple(jax.ShapeDtypeStruct(r.shape, f32) for r in results),
+        in_specs=[any_space] * 2,
+        out_specs=(any_space,) * 2,
+        scratch_shapes=[vmem(les_state.shape, f32), vmem(wave_state.shape, f32), dma((6,)), dma((6,))],
+        name="hand_on",
+    )(*results)
 
 
 def solution(mesh):

time: 57 us -> 50.8 us (0.89)
  Pallas kernels: 53.3 us -> 49.8 us
  local copies, waits for them, and re-layouts: 2.85 us -> 0 us
    pallas_call x1, Pallas kernels: 53.3 us -> 47.7 us  [on_device(): pl.pallas_call(functools.partial(kernel, sizes, far_order), out_shape=(ja...]
    unnamed x4 -> x0, local copies, waits for them, and re-layouts: 2.85 us -> none
    pallas_call x0 -> x1, Pallas kernels: none -> 2.08 us  [on_device(): pl.pallas_call(hand_on, out_shape=tuple((jax.ShapeDtypeStruct(r.shape, f3...]
where the time goes in v2:
time: 50.8 us; the launch traced here: 50.4 us
  Pallas kernels  49.8 us (98%)
  between operations  0.64 us (1%)
    pallas_call x1, Pallas kernels, on_device(): pl.pallas_call(functools.partial(kernel, sizes, far_order), out_shape=(ja...  47.7 us
    pallas_call x1, Pallas kernels, on_device(): pl.pallas_call(hand_on, out_shape=tuple((jax.ShapeDtypeStruct(r.shape, f3...  2.08 us

profile of v2, /device:TPU:1, one launch (start us, length us, event | category | flops | bytes accessed | tf_op | source)
XLA Modules:
  0.0 50.4 jit_solution(10162771525364779848)
XLA Ops:
  0.6 47.7 %jet_step.1 = (f32[5,8,48,128]{3,2,1,0:T(8,128)}, f32[3,8,128]{2,1,0:T(8,128)}) custom-call(f32[5,8,48,128]{3,2,1,0:T(8,128)} %les_ref.1, f32[3,8,128]{2,1,0:T(8,128)} %wave_in.1, bf16[6144,128]{1,0:T(8,128)(2,1)} %bitcast.4, s32[1,4,8]{2,1,0:T(4,128)} %bitcast.5, s32[1,4,8]{2,1,0:T(4,128)} %bitcast.6, s32[1,4,8]{2,1,0:T(4,128)} %bitcast.7, s32[1,8]{1,0:T(1,128)} %mask_in.1), custom_call_target="tpu_custom_call" | custom-call | tf_op jit(solution)/shard_map/jet_step/pallas_call | solution.py:597
  48.4 2.1 %hand_on.1 = (f32[5,8,48,128]{3,2,1,0:T(8,128)}, f32[3,8,128]{2,1,0:T(8,128)}) custom-call(f32[5,8,48,128]{3,2,1,0:T(8,128)} %get-tuple-element.4.les_in, f32[3,8,128]{2,1,0:T(8,128)} %get-tuple-element.5.wave_in), custom_call_target="tpu_custom_call" | custom-call | tf_op jit(solution)/shard_map/hand_on/pallas_call | solution.py:609

commit v3 on v2

--- a/solution.py
+++ b/solution.py
@@ -13,6 +13,9 @@
 WAVE_STEP = 0.3
 CX, CZ, CY = 8, 48, 128
 ZT = CZ // 8
+CHUNKS = 3
+CHUNK_ROWS = CZ // CHUNKS
+CHUNK_TILES = ZT // CHUNKS
 OFFSETS = (1.0, 0.0, 0.0, 0.0, 1.0)
 STATE_SCALE = (130816.0, 65408.0, 65408.0, 65408.0, 130816.0)
 PRED_SCALE = (24576.0,) * 5
@@ -125,7 +128,7 @@
     wave_ref, owner_ref, slot_ref, weight_ref, mask_ref,
     xs1, xr1, xs2, xr2, zs1, zr1, zs2, zr2, ys1, yr1, ys2, yr2, ym2,
     exz_s, exz_r, ezy_s, ezy_r, ezy_x,
-    light, ops_raw, ops_wide, ops_mat, spread, weight_tiles,
+    light, ops_raw, ops_wide, ops_mat, spread, labels, weight_tiles,
     sent, received, own_source, near_source, near_wave,
     local_sems, x_send, x_recv, send1, recv1, send2, recv2, wave_send, wave_recv, all_send, all_recv, src_send, src_recv, gossip,
 ):
@@ -179,7 +182,7 @@
             pl.semaphore_wait(gossip.at[r], 2)
 
     def x_pack(buf, out, scales, chunk):
-        part = slice(8 + 24 * chunk, 32 + 24 * chunk)
+        part = slice(8 + CHUNK_ROWS * chunk, 8 + CHUNK_ROWS * (chunk + 1))
         for f in range(5):
             for side, first in ((0, 2), (1, 8)):
                 out[side, chunk, f] = pair_words(
@@ -187,7 +190,7 @@
                 )
 
     def x_unpack(buf, words, scales, chunk):
-        part = slice(8 + 24 * chunk, 32 + 24 * chunk)
+        part = slice(8 + CHUNK_ROWS * chunk, 8 + CHUNK_ROWS * (chunk + 1))
         for f in range(5):
             for side, first in ((0, 0), (1, 10)):
                 one, two = split_words(words[side, chunk, f], OFFSETS[f], scales[f])
@@ -195,7 +198,7 @@
                 buf[f, first + 1, part, :] = two
 
     def x_copies(sent_words, words, stage, chunk):
-        first = 4 * stage + 2 * chunk
+        first = 2 * (CHUNKS * stage + chunk)
         return [
             remote(
                 sent_words.at[0, chunk], words.at[1, chunk], x_send.at[first], x_recv.at[first + 1], (g, gx_low, gy)
@@ -241,8 +244,8 @@
     x_pack(state, xs1, STATE_SCALE, 0)
     pl.semaphore_wait(barrier, 5)
     gossip_send(0)
-    x_first = [x_copies(xs1, xr1, 0, chunk) for chunk in range(2)]
-    x_second = [x_copies(xs2, xr2, 1, chunk) for chunk in range(2)]
+    x_first = [x_copies(xs1, xr1, 0, chunk) for chunk in range(CHUNKS)]
+    x_second = [x_copies(xs2, xr2, 1, chunk) for chunk in range(CHUNKS)]
     first = [
         remote(zs1, zr1, send1.at[0], recv1.at[0], (other, gx, gy)),
         remote(ys1, yr1.at[1], send1.at[1], recv1.at[2], (g, gx, gy_low)),
@@ -250,9 +253,10 @@
     ]
     for copy in x_first[0]:
         copy.start()
-    x_pack(state, xs1, STATE_SCALE, 1)
-    for copy in x_first[1]:
-        copy.start()
+    for chunk in range(1, CHUNKS):
+        x_pack(state, xs1, STATE_SCALE, chunk)
+        for copy in x_first[chunk]:
+            copy.start()
     load_inner.wait()
     z_pack(state, zs1, STATE_SCALE)
     first[0].start()
@@ -274,16 +278,35 @@
         return carry
 
     lax.fori_loop(0, 12, widen, 0)
-    target = jnp.full((8, 128), -1, jnp.int32)
+    pair_lane = lane & 31
+    owners = jnp.full((8, 128), -99, jnp.int32)
+    first_slot, second_slot, seen = (jnp.zeros((8, 128), jnp.int32) for _ in range(3))
     for k in range(4):
         weights = jnp.zeros((8, 128), jnp.int32)
         for x in range(8):
-            line = owner_ref[0, k, x] * 8 + slot_ref[0, k, x]
-            target = jnp.where(((lane & 31) == k * 8 + x) & (lane < 96), line, target)
+            owner = owner_ref[0, k, x]
+            owners = jnp.where((pair_lane == k * 8 + x) & (lane < 96), owner, owners)
+            hit = lane == owner
+            first_slot = jnp.where(hit & (seen == 0), slot_ref[0, k, x] + 1, first_slot)
+            second_slot = jnp.where(hit & (seen == 1), slot_ref[0, k, x] + 1, second_slot)
+            seen = jnp.where(hit, seen + 1, seen)
             weights = jnp.where(row == x, weight_ref[0, k, x], weights)
         weight_tiles[k] = weights
-    for o in range(n_gx):
-        spread[o * 8:(o + 1) * 8, :] = jnp.where(target == row + o * 8, 1.0, 0.0)
+    rank_of = jnp.zeros((8, 128), jnp.int32)
+    for k in range(4):
+        for x in range(8):
+            earlier = (owners == owner_ref[0, k, x]) & (pair_lane > k * 8 + x)
+            rank_of = rank_of + jnp.where(earlier, 1, 0)
+    own_lane = 8 * lax.rem(gx, 16)
+    first_slot = pltpu.roll(first_slot.astype(jnp.float32), own_lane + 1, 1)
+    second_slot = pltpu.roll(second_slot.astype(jnp.float32), own_lane + 5, 1)
+    first_here = (row == 7) & (lane >= own_lane) & (lane < own_lane + 3)
+    second_here = (row == 7) & (lane >= own_lane + 4) & (lane < own_lane + 7)
+    for d in range(n_gx):
+        near = (owners >= d - 1) & (owners <= d + 1)
+        spread[d * 8:(d + 1) * 8, :] = jnp.where(near & (owners - (d - 1) + 4 * rank_of == row), 1.0, 0.0)
+        slots = jnp.where(second_here, roll_lane(second_slot, -d), 0.0)
+        labels[d * 8:(d + 1) * 8, :] = jnp.where(first_here, roll_lane(first_slot, -d), slots)
 
     gossip_wait(0)
     gossip_send(1)
@@ -323,16 +346,12 @@
     lax.fori_loop(2, 6, rate_inner, 0)
     gossip_wait(1)
     gossip_send(2)
-    for chunk in range(2):
+    for chunk in range(CHUNKS):
         for copy in x_first[chunk]:
             copy.wait_recv()
         x_unpack(state, xr1, STATE_SCALE, chunk)
-
-        def rate_outer(j, carry):
-            first_rate(lax.rem(j + 6, 8), tuple(range(3 * chunk, 3 * chunk + 3)))
-            return carry
-
-        lax.fori_loop(0, 4, rate_outer, 0)
+        for x in (6, 7, 0, 1):
+            first_rate(x, tuple(range(CHUNK_TILES * chunk, CHUNK_TILES * (chunk + 1))))
         x_pack(pred, xs2, PRED_SCALE, chunk)
         for copy in x_second[chunk]:
             copy.start()
@@ -415,7 +434,7 @@
         return carry
 
     lax.fori_loop(2, 6, lighthill, 0)
-    for chunk in range(2):
+    for chunk in range(CHUNKS):
         for copy in x_second[chunk]:
             copy.wait_recv()
         x_unpack(pred, xr2, PRED_SCALE, chunk)
@@ -461,7 +480,7 @@
     middle = (values - high).astype(jnp.bfloat16).astype(jnp.float32)
     rest = values - high - middle
     stacked = jnp.concatenate([high, middle, rest, jnp.zeros((32, 128), jnp.float32)], axis=0).astype(jnp.bfloat16)
-    sent[...] = jnp.dot(spread[...].astype(jnp.bfloat16), stacked, preferred_element_type=jnp.float32)
+    sent[...] = labels[...] + jnp.dot(spread[...].astype(jnp.bfloat16), stacked, preferred_element_type=jnp.float32)
 
     gossip_wait(3)
     all_copies = []
@@ -503,11 +522,21 @@
 
     others = received.at[0:n_gx - 1]
     pltpu.make_async_copy(others, others, all_recv.at[0]).wait()
-    own_source[...] = jnp.sum(received[...], axis=0)
-    for dx, dr in around:
-        remote(
-            own_source, near_source.at[slot_of(-dx, -dr)], src_send.at[0], src_recv.at[0], neighbour(dx, dr)
-        ).start()
+    tags = jnp.concatenate([jnp.sum(received[h:h + 16], axis=0)[7:8, :] for h in (0, 16)], axis=1)
+    tags = jnp.broadcast_to(tags, (24, 256))
+    line = lax.broadcasted_iota(jnp.int32, (24, 256), 0)
+    column = lax.broadcasted_iota(jnp.int32, (24, 256), 1)
+    lands = tags + (8 * (column & 3) - 1 - line).astype(jnp.float32)
+    gather = jnp.where((tags > 0.5) & (jnp.abs(lands) < 0.5), 1.0, 0.0).astype(jnp.bfloat16)
+    arrived = received[...].reshape(n_gx * 8, 128)
+    high = arrived.astype(jnp.bfloat16).astype(jnp.float32)
+    middle = (arrived - high).astype(jnp.bfloat16).astype(jnp.float32)
+    source_lines = jnp.zeros((24, 128), jnp.float32)
+    for part in (arrived - high - middle, middle, high):
+        source_lines = source_lines + jnp.dot(gather, part.astype(jnp.bfloat16), preferred_element_type=jnp.float32)
+    own_source[...] = source_lines
+    for i, dr in ((0, -1), (1, 1)):
+        remote(own_source, near_source.at[1 - i], src_send.at[0], src_recv.at[0], neighbour(0, dr)).start()
 
     pltpu.make_async_copy(near_wave, near_wave, wave_recv.at[0]).wait()
     wide_row = lax.broadcasted_iota(jnp.int32, (24, 256), 0)
@@ -535,7 +564,8 @@
 
     now = [assemble(wave_block(f)) for f in range(3)]
     pltpu.make_async_copy(near_source, near_source, src_recv.at[0]).wait()
-    source = assemble(lambda dx, dr: own_source[...] if (dx, dr) == (0, 0) else near_source[slot_of(dx, dr)])
+    beside = jnp.where(wide_lane[:, 0:128] < 64, near_source[1], near_source[0])
+    source = jnp.concatenate([own_source[...], beside], axis=1) * inside
     for _ in range(2):
         rate_one = wave_rates(now, source, inverse_radius)
         ahead = [(v + WAVE_STEP * r) * inside for v, r in zip(now, rate_one)]
@@ -544,7 +574,7 @@
     for f in range(3):
         wave_out[f] = now[f][8:16, 0:128]
 
-    for copy in first + second + x_first[0] + x_first[1] + x_second[0] + x_second[1]:
+    for copy in sum(x_first + x_second, first + second):
         copy.wait_send()
     pltpu.make_async_copy(others, others, all_send.at[0]).wait()
     pltpu.make_async_copy(near_wave, near_wave, wave_send.at[0]).wait()
@@ -578,18 +608,18 @@
         vmem((12, 48, 128), f32), vmem((8, 64, 128), f32), vmem((8, 48, 128), f32),
         vmem((10, 64, 128), f32), vmem((10, 48, 128), f32), vmem((8, 64, 128), f32),
         vmem((3, 8, 128), f32), smem((1, 4, 8), i32), smem((1, 4, 8), i32), smem((1, 4, 8), i32), smem((1, 8), i32),
-        vmem((2, 2, 5, 24, 128), i32), vmem((2, 2, 5, 24, 128), i32),
-        vmem((2, 2, 5, 24, 128), i32), vmem((2, 2, 5, 24, 128), i32),
+        vmem((2, CHUNKS, 5, CHUNK_ROWS, 128), i32), vmem((2, CHUNKS, 5, CHUNK_ROWS, 128), i32),
+        vmem((2, CHUNKS, 5, CHUNK_ROWS, 128), i32), vmem((2, CHUNKS, 5, CHUNK_ROWS, 128), i32),
         vmem((10, 8, 128), i32), vmem((10, 8, 128), i32), vmem((10, 8, 128), i32), vmem((10, 8, 128), i32),
         vmem((8, 8, 128), f32), vmem((2, 8, 8, 128), f32), vmem((8, 8, 128), f32), vmem((2, 10, 8, 128), f32),
         vmem((10, 8, 128), f32),
         vmem((2, 8, 128), f32), vmem((2, 8, 128), f32), vmem((8, 128), f32), vmem((2, 8, 128), f32),
         vmem((8, 8, 128), f32),
         vmem((CX * CZ, 128), f32), vmem((6144, 128), bf16), vmem((512, 128), f32), vmem((1536, 512), bf16),
-        vmem((n_gx * 8, 128), f32), vmem((4, 8, 128), i32),
-        vmem((n_gx * 8, 128), f32), vmem((n_gx, 8, 128), f32), vmem((8, 128), f32),
-        vmem((8, 8, 128), f32), vmem((8, 3, 8, 128), f32),
-        dma((9,)), dma((8,)), dma((8,)), dma((3,)), dma((3,)), dma((11,)), dma((11,)), dma((1,)), dma((1,)), dma((1,)), dma((1,)),
+        vmem((n_gx * 8, 128), f32), vmem((n_gx * 8, 128), f32), vmem((4, 8, 128), i32),
+        vmem((n_gx * 8, 128), f32), vmem((n_gx, 8, 128), f32), vmem((24, 128), f32),
+        vmem((2, 24, 128), f32), vmem((8, 3, 8, 128), f32),
+        dma((9,)), dma((4 * CHUNKS,)), dma((4 * CHUNKS,)), dma((3,)), dma((3,)), dma((11,)), dma((11,)), dma((1,)), dma((1,)), dma((1,)), dma((1,)),
         dma((1,)), dma((1,)), pltpu.SemaphoreType.REGULAR((rounds,)),
     ]
     any_space = pl.BlockSpec(memory_space=pl.ANY)

time: 50.8 us -> 47.7 us (0.939)
  Pallas kernels: 49.8 us -> 46.9 us
    pallas_call x1, Pallas kernels: 47.7 us -> 44.8 us  [on_device(): pl.pallas_call(functools.partial(kernel, sizes, far_order), out_shape=(ja...]
where the time goes in v3:
time: 47.7 us; the launch traced here: 47.5 us
  Pallas kernels  46.9 us (98%)
  between operations  0.64 us (1%)
    pallas_call x1, Pallas kernels, on_device(): pl.pallas_call(functools.partial(kernel, sizes, far_order), out_shape=(ja...  44.8 us
    pallas_call x1, Pallas kernels, on_device(): pl.pallas_call(hand_on, out_shape=tuple((jax.ShapeDtypeStruct(r.shape, f3...  2.08 us

profile of v3, /device:TPU:1, one launch (start us, length us, event | category | flops | bytes accessed | tf_op | source)
XLA Modules:
  0.0 47.5 jit_solution(3082561412970412190)
XLA Ops:
  0.6 44.8 %jet_step.1 = (f32[5,8,48,128]{3,2,1,0:T(8,128)}, f32[3,8,128]{2,1,0:T(8,128)}) custom-call(f32[5,8,48,128]{3,2,1,0:T(8,128)} %les_ref.1, f32[3,8,128]{2,1,0:T(8,128)} %wave_in.1, bf16[6144,128]{1,0:T(8,128)(2,1)} %bitcast.4, s32[1,4,8]{2,1,0:T(4,128)} %bitcast.5, s32[1,4,8]{2,1,0:T(4,128)} %bitcast.6, s32[1,4,8]{2,1,0:T(4,128)} %bitcast.7, s32[1,8]{1,0:T(1,128)} %mask_in.1), custom_call_target="tpu_custom_call" | custom-call | tf_op jit(solution)/shard_map/jet_step/pallas_call | solution.py:627
  45.5 2.1 %hand_on.1 = (f32[5,8,48,128]{3,2,1,0:T(8,128)}, f32[3,8,128]{2,1,0:T(8,128)}) custom-call(f32[5,8,48,128]{3,2,1,0:T(8,128)} %get-tuple-element.4.les_in, f32[3,8,128]{2,1,0:T(8,128)} %get-tuple-element.5.wave_in), custom_call_target="tpu_custom_call" | custom-call | tf_op jit(solution)/shard_map/hand_on/pallas_call | solution.py:639

commit v4 on v3

--- a/solution.py
+++ b/solution.py
@@ -155,20 +155,30 @@
         copy.start()
         return copy
 
-    load_faces = [
-        load(les_ref.at[:, 0:2], state.at[:, 2:4, 8:56, :], 0),
-        load(les_ref.at[:, 6:8], state.at[:, 8:10, 8:56, :], 1),
+    def face_rows(chunk):
+        return slice(CHUNK_ROWS * chunk, CHUNK_ROWS * (chunk + 1)), slice(
+            8 + CHUNK_ROWS * chunk, 8 + CHUNK_ROWS * (chunk + 1)
+        )
+
+    load_faces = []
+    for chunk in range(CHUNKS):
+        theirs, mine = face_rows(chunk)
+        load_faces.append(
+            [
+                load(les_ref.at[:, 0:2, theirs], state.at[:, 2:4, mine, :], 7 + 2 * chunk),
+                load(les_ref.at[:, 6:8, theirs], state.at[:, 8:10, mine, :], 8 + 2 * chunk),
+            ]
+        )
+    load_inner = load(les_ref.at[:, 2:6], state.at[:, 4:8, 8:56, :], 0)
+    load_small = [
+        load(owner_in, owner_ref, 1),
+        load(slot_in, slot_ref, 2),
+        load(weight_in, weight_ref, 3),
+        load(mask_in, mask_ref, 4),
+        load(wave_in, wave_ref, 5),
     ]
-    load_inner = load(les_ref.at[:, 2:6], state.at[:, 4:8, 8:56, :], 2)
-    load_small = [
-        load(owner_in, owner_ref, 3),
-        load(slot_in, slot_ref, 4),
-        load(weight_in, weight_ref, 5),
-        load(mask_in, mask_ref, 6),
-        load(wave_in, wave_ref, 7),
-    ]
-    load_ops = load(ops_ref, ops_raw, 8)
-    for copy in load_faces:
+    load_ops = load(ops_ref, ops_raw, 6)
+    for copy in load_faces[0]:
         copy.wait()
 
     def gossip_send(r):
@@ -254,6 +264,8 @@
     for copy in x_first[0]:
         copy.start()
     for chunk in range(1, CHUNKS):
+        for copy in load_faces[chunk]:
+            copy.wait()
         x_pack(state, xs1, STATE_SCALE, chunk)
         for copy in x_first[chunk]:
             copy.start()
@@ -343,19 +355,6 @@
         first_rate(x, tuple(range(ZT)))
         return carry
 
-    lax.fori_loop(2, 6, rate_inner, 0)
-    gossip_wait(1)
-    gossip_send(2)
-    for chunk in range(CHUNKS):
-        for copy in x_first[chunk]:
-            copy.wait_recv()
-        x_unpack(state, xr1, STATE_SCALE, chunk)
-        for x in (6, 7, 0, 1):
-            first_rate(x, tuple(range(CHUNK_TILES * chunk, CHUNK_TILES * (chunk + 1))))
-        x_pack(pred, xs2, PRED_SCALE, chunk)
-        for copy in x_second[chunk]:
-            copy.start()
-
     second = [
         remote(zs2, zr2, send2.at[0], recv2.at[0], (other, gx, gy)),
         remote(ys2, yr2.at[1, 1:9], send2.at[1], recv2.at[2], (g, gx, gy_low)),
@@ -369,11 +368,25 @@
         remote(ys2.at[7], yr2.at[1, 0], send2.at[9], recv2.at[8], (g, gx_high, gy_low)),
         remote(ys2.at[7], yr2.at[0, 0], send2.at[10], recv2.at[7], (g, gx_high, gy_high)),
     ]
-    for side in range(2):
-        x = 7 * side
-        exz_s[side] = ends(pred, 0, x) * ends(pred, 1, x) * ends(pred, 2, x)
-    for copy in second[5:]:
-        copy.start()
+    lax.fori_loop(2, 6, rate_inner, 0)
+    gossip_wait(1)
+    gossip_send(2)
+    for chunk in range(CHUNKS):
+        for copy in x_first[chunk]:
+            copy.wait_recv()
+        x_unpack(state, xr1, STATE_SCALE, chunk)
+        for x in (6, 7, 0, 1):
+            first_rate(x, tuple(range(CHUNK_TILES * chunk, CHUNK_TILES * (chunk + 1))))
+        if chunk == CHUNKS - 1:
+            for side in range(2):
+                x = 7 * side
+                exz_s[side] = ends(pred, 0, x) * ends(pred, 1, x) * ends(pred, 2, x)
+            for copy in second[5:]:
+                copy.start()
+        x_pack(pred, xs2, PRED_SCALE, chunk)
+        for copy in x_second[chunk]:
+            copy.start()
+
     z_pack(pred, zs2, PRED_SCALE)
     for copy in second[:3]:
         copy.start()
@@ -513,12 +526,10 @@
             _, rates = rate_tile(pred, x, zt, halo)
             part = pl.ds(8 * zt, 8)
             for f in range(5):
-                base_sum[f, x, part, :] = base_sum[f, x, part, :] + (0.5 * LES_STEP) * rates[f]
+                les_out[f, x, part, :] = base_sum[f, x, part, :] + (0.5 * LES_STEP) * rates[f]
         return carry
 
     lax.fori_loop(0, CX, second_rate, 0)
-    store_les = pltpu.make_async_copy(base_sum, les_out, local_sems.at[0])
-    store_les.start()
 
     others = received.at[0:n_gx - 1]
     pltpu.make_async_copy(others, others, all_recv.at[0]).wait()
@@ -579,19 +590,14 @@
     pltpu.make_async_copy(others, others, all_send.at[0]).wait()
     pltpu.make_async_copy(near_wave, near_wave, wave_send.at[0]).wait()
     pltpu.make_async_copy(near_source, near_source, src_send.at[0]).wait()
-    store_les.wait()
-
-
-def hand_on(les_in, wave_in, les_out, wave_out, les_buf, wave_buf, in_sems, out_sems):
-    legs = [(wave_in, wave_buf, wave_out)] + [(les_in.at[f], les_buf.at[f], les_out.at[f]) for f in range(5)]
-    into = [pltpu.make_async_copy(a, b, in_sems.at[i]) for i, (a, b, _) in enumerate(legs)]
-    out = [pltpu.make_async_copy(b, c, out_sems.at[i]) for i, (_, b, c) in enumerate(legs)]
-    for copy in into:
+
+
+def hand_on(les_in, wave_in, les_out, wave_out, sems):
+    copies = [pltpu.make_async_copy(wave_in, wave_out, sems.at[5])]
+    copies += [pltpu.make_async_copy(les_in.at[f], les_out.at[f], sems.at[f]) for f in range(5)]
+    for copy in copies:
         copy.start()
-    for one, two in zip(into, out):
-        one.wait()
-        two.start()
-    for copy in out:
+    for copy in copies:
         copy.wait()
 
 
@@ -619,19 +625,16 @@
         vmem((n_gx * 8, 128), f32), vmem((n_gx * 8, 128), f32), vmem((4, 8, 128), i32),
         vmem((n_gx * 8, 128), f32), vmem((n_gx, 8, 128), f32), vmem((24, 128), f32),
         vmem((2, 24, 128), f32), vmem((8, 3, 8, 128), f32),
-        dma((9,)), dma((4 * CHUNKS,)), dma((4 * CHUNKS,)), dma((3,)), dma((3,)), dma((11,)), dma((11,)), dma((1,)), dma((1,)), dma((1,)), dma((1,)),
+        dma((7 + 2 * CHUNKS,)), dma((4 * CHUNKS,)), dma((4 * CHUNKS,)), dma((3,)), dma((3,)), dma((11,)), dma((11,)), dma((1,)), dma((1,)), dma((1,)), dma((1,)),
         dma((1,)), dma((1,)), pltpu.SemaphoreType.REGULAR((rounds,)),
     ]
     any_space = pl.BlockSpec(memory_space=pl.ANY)
     in_vmem = pl.BlockSpec(memory_space=pltpu.VMEM)
     results = pl.pallas_call(
         functools.partial(kernel, sizes, far_order),
-        out_shape=(
-            jax.ShapeDtypeStruct(les_state.shape, f32),
-            jax.ShapeDtypeStruct(wave_state.shape, f32),
-        ),
+        out_shape=(vmem(les_state.shape, f32), vmem(wave_state.shape, f32)),
         in_specs=[any_space] * 7,
-        out_specs=(any_space, in_vmem),
+        out_specs=(in_vmem, in_vmem),
         scratch_shapes=scratch,
         compiler_params=pltpu.CompilerParams(collective_id=0, has_side_effects=True),
         name="jet_step",
@@ -639,11 +642,11 @@
     return pl.pallas_call(
         hand_on,
         out_shape=tuple(jax.ShapeDtypeStruct(r.shape, f32) for r in results),
-        in_specs=[any_space] * 2,
+        in_specs=[in_vmem] * 2,
         out_specs=(any_space,) * 2,
-        scratch_shapes=[vmem(les_state.shape, f32), vmem(wave_state.shape, f32), dma((6,)), dma((6,))],
+        scratch_shapes=[dma((6,))],
         name="hand_on",
-    )(*results)
+    )(*(pltpu.with_memory_space_constraint(r, pltpu.VMEM) for r in results))
 
 
 def solution(mesh):

time: 47.7 us -> 46.3 us (0.971)
  Pallas kernels: 46.9 us -> 45.6 us
    pallas_call x1, Pallas kernels: 2.08 us -> 0.99 us  [on_device(): pl.pallas_call(hand_on, out_shape=tuple((jax.ShapeDtypeStruct(r.shape, f3...]
where the time goes in v4:
time: 46.3 us; the launch traced here: 46.2 us
  Pallas kernels  45.6 us (98%)
  between operations  0.64 us (1%)
    pallas_call x1, Pallas kernels, on_device(): pl.pallas_call(functools.partial(kernel, sizes, far_order), out_shape=(vm...  44.6 us
    pallas_call x1, Pallas kernels, on_device(): pl.pallas_call(hand_on, out_shape=tuple((jax.ShapeDtypeStruct(r.shape, f3...  0.99 us

profile of v4, /device:TPU:1, one launch (start us, length us, event | category | flops | bytes accessed | tf_op | source)
XLA Modules:
  0.0 46.2 jit_solution(9949613585953246537)
XLA Ops:
  0.6 44.6 %jet_step.1 = (f32[5,8,48,128]{3,2,1,0:T(8,128)S(1)}, f32[3,8,128]{2,1,0:T(8,128)S(1)}) custom-call(f32[5,8,48,128]{3,2,1,0:T(8,128)} %les_ref.1, f32[3,8,128]{2,1,0:T(8,128)} %wave_in.1, bf16[6144,128]{1,0:T(8,128)(2,1)} %bitcast.4, s32[1,4,8]{2,1,0:T(4,128)} %bitcast.5, s32[1,4,8]{2,1,0:T(4,128)} %bitcast.6, s32[1,4,8]{2,1,0:T(4,128)} %bitcast.7, ...), custom_call_target="tpu_custom_call" | custom-call | tf_op jit(solution)/shard_map/jet_step/pallas_call | solution.py:633
  45.2 1.0 %hand_on.1 = (f32[5,8,48,128]{3,2,1,0:T(8,128)}, f32[3,8,128]{2,1,0:T(8,128)}) custom-call(f32[5,8,48,128]{3,2,1,0:T(8,128)S(1)} %get-tuple-element.4.les_in, f32[3,8,128]{2,1,0:T(8,128)S(1)} %get-tuple-element.5.wave_in), custom_call_target="tpu_custom_call" | custom-call | tf_op jit(solution)/shard_map/hand_on/pallas_call | solution.py:642

commit v5 on v4

--- a/solution.py
+++ b/solution.py
@@ -369,6 +369,23 @@
         remote(ys2.at[7], yr2.at[0, 0], send2.at[10], recv2.at[7], (g, gx_high, gy_high)),
     ]
     lax.fori_loop(2, 6, rate_inner, 0)
+
+    around = [(dx, dr) for dx in (-1, 0, 1) for dr in (-1, 0, 1) if (dx, dr) != (0, 0)]
+
+    def neighbour(dx, dr):
+        there = lax.rem(rank + (n_rank + dr), n_rank)
+        return (there // n_gy, lax.rem(gx + (n_gx + dx), n_gx), lax.rem(there, n_gy))
+
+    def slot_of(dx, dr):
+        return around.index((dx, dr))
+
+    def send_wave(corner):
+        for dx, dr in around:
+            if (dx * dr != 0) == corner:
+                slot = near_wave.at[slot_of(-dx, -dr)]
+                remote(wave_ref, slot, wave_send.at[0], wave_recv.at[0], neighbour(dx, dr)).start()
+
+    send_wave(False)
     gossip_wait(1)
     gossip_send(2)
     for chunk in range(CHUNKS):
@@ -457,6 +474,7 @@
         m0 = pred[0, layer, 8:56, :] * pred[1, layer, 8:56, :]
         s01[index, 8:56, :] = m0 * pred[2, layer, 8:56, :]
         s02[index] = m0 * pred[3, layer, 8:56, :]
+    send_wave(True)
     for copy in second[5:]:
         copy.wait_recv()
     for index in (0, 9):
@@ -506,20 +524,6 @@
         copy.start()
     received[gx] = sent[pl.ds(pl.multiple_of(gx * 8, 8), 8), :]
 
-    around = [(dx, dr) for dx in (-1, 0, 1) for dr in (-1, 0, 1) if (dx, dr) != (0, 0)]
-
-    def neighbour(dx, dr):
-        there = lax.rem(rank + (n_rank + dr), n_rank)
-        return (there // n_gy, lax.rem(gx + (n_gx + dx), n_gx), lax.rem(there, n_gy))
-
-    def slot_of(dx, dr):
-        return around.index((dx, dr))
-
-    for dx, dr in around:
-        remote(
-            wave_ref, near_wave.at[slot_of(-dx, -dr)], wave_send.at[0], wave_recv.at[0], neighbour(dx, dr)
-        ).start()
-
     def second_rate(x, carry):
         halo = ym2[x + 1]
         for zt in range(ZT):
@@ -574,11 +578,16 @@
         return lambda dx, dr: wave_ref[f] if (dx, dr) == (0, 0) else near_wave[slot_of(dx, dr), f]
 
     now = [assemble(wave_block(f)) for f in range(3)]
+    no_source = jnp.zeros((24, 256), jnp.float32)
+    opening = wave_rates(now, no_source, inverse_radius)
     pltpu.make_async_copy(near_source, near_source, src_recv.at[0]).wait()
     beside = jnp.where(wide_lane[:, 0:128] < 64, near_source[1], near_source[0])
     source = jnp.concatenate([own_source[...], beside], axis=1) * inside
-    for _ in range(2):
-        rate_one = wave_rates(now, source, inverse_radius)
+    for step in range(2):
+        if step == 0:
+            rate_one = (opening[0] + source, opening[1], opening[2])
+        else:
+            rate_one = wave_rates(now, source, inverse_radius)
         ahead = [(v + WAVE_STEP * r) * inside for v, r in zip(now, rate_one)]
         rate_two = wave_rates(ahead, source, inverse_radius)
         now = [(v + (0.5 * WAVE_STEP) * (a + b)) * inside for v, a, b in zip(now, rate_one, rate_two)]

time: 46.3 us -> 46.1 us (level)
  no operation moved by 1% of the time
where the time goes in v5:
time: 46.1 us; the launch traced here: 45.9 us
  Pallas kernels  45.3 us (98%)
  between operations  0.64 us (1%)
    pallas_call x1, Pallas kernels, on_device(): pl.pallas_call(functools.partial(kernel, sizes, far_order), out_shape=(vm...  44.3 us
    pallas_call x1, Pallas kernels, on_device(): pl.pallas_call(hand_on, out_shape=tuple((jax.ShapeDtypeStruct(r.shape, f3...  0.99 us

profile of v5, /device:TPU:1, one launch (start us, length us, event | category | flops | bytes accessed | tf_op | source)
XLA Modules:
  0.0 45.9 jit_solution(14855045772082693623)
XLA Ops:
  0.6 44.3 %jet_step.1 = (f32[5,8,48,128]{3,2,1,0:T(8,128)S(1)}, f32[3,8,128]{2,1,0:T(8,128)S(1)}) custom-call(f32[5,8,48,128]{3,2,1,0:T(8,128)} %les_ref.1, f32[3,8,128]{2,1,0:T(8,128)} %wave_in.1, bf16[6144,128]{1,0:T(8,128)(2,1)} %bitcast.4, s32[1,4,8]{2,1,0:T(4,128)} %bitcast.5, s32[1,4,8]{2,1,0:T(4,128)} %bitcast.6, s32[1,4,8]{2,1,0:T(4,128)} %bitcast.7, ...), custom_call_target="tpu_custom_call" | custom-call | tf_op jit(solution)/shard_map/jet_step/pallas_call | solution.py:642
  44.9 1.0 %hand_on.1 = (f32[5,8,48,128]{3,2,1,0:T(8,128)}, f32[3,8,128]{2,1,0:T(8,128)}) custom-call(f32[5,8,48,128]{3,2,1,0:T(8,128)S(1)} %get-tuple-element.4.les_in, f32[3,8,128]{2,1,0:T(8,128)S(1)} %get-tuple-element.5.wave_in), custom_call_target="tpu_custom_call" | custom-call | tf_op jit(solution)/shard_map/hand_on/pallas_call | solution.py:651

commit v6 on v5

--- a/solution.py
+++ b/solution.py
@@ -435,7 +435,7 @@
     for x in range(8):
         ezy_x[x] = roll_lane(corners, -8 * x)
 
-    def lighthill(x, carry):
+    def lighthill(x, tiles):
         along_x = packed_products(ym2[x + 2])[0] - packed_products(ym2[x])[0]
         _, s12_halo, square = packed_products(ym2[x + 1])
         corner = ezy_x[x]
@@ -445,7 +445,7 @@
         before = roll_row(jnp.where(row == 7, last_tile, s12_halo), 1)
         cross = along_x + (after - before)
         keep = mask_ref[0, x].astype(jnp.float32)
-        for zt in range(ZT):
+        for zt in tiles:
             part = pl.ds(8 * zt, 8)
 
             def z(ref, index, dz):
@@ -461,28 +461,34 @@
             ((before, after),) = y_shifts(tile, cross, zt, (1,))
             mixed = mixed + (after - before)
             light[pl.ds(pl.multiple_of(x * CZ + 8 * zt, 8), 8), :] = (0.25 * direct + 0.5 * mixed) * keep
-        return carry
-
-    lax.fori_loop(2, 6, lighthill, 0)
+        return 0
+
+    lax.fori_loop(2, 6, lambda x, carry: lighthill(x, range(ZT)), 0)
     for chunk in range(CHUNKS):
         for copy in x_second[chunk]:
             copy.wait_recv()
         x_unpack(pred, xr2, PRED_SCALE, chunk)
-    for index in (0, 1, 10, 11):
-        s00[index] = pred[0, index, 8:56, :] * pred[1, index, 8:56, :] * pred[1, index, 8:56, :]
-    for index, layer in ((0, 1), (9, 10)):
-        m0 = pred[0, layer, 8:56, :] * pred[1, layer, 8:56, :]
-        s01[index, 8:56, :] = m0 * pred[2, layer, 8:56, :]
-        s02[index] = m0 * pred[3, layer, 8:56, :]
+        part = slice(CHUNK_ROWS * chunk, CHUNK_ROWS * (chunk + 1))
+        inner = slice(8 + CHUNK_ROWS * chunk, 8 + CHUNK_ROWS * (chunk + 1))
+        for index in (0, 1, 10, 11):
+            s00[index, part, :] = pred[0, index, inner, :] * pred[1, index, inner, :] * pred[1, index, inner, :]
+        for index, layer in ((0, 1), (9, 10)):
+            m0 = pred[0, layer, inner, :] * pred[1, layer, inner, :]
+            s01[index, inner, :] = m0 * pred[2, layer, inner, :]
+            s02[index, part, :] = m0 * pred[3, layer, inner, :]
+        if chunk == CHUNKS - 2:
+            for copy in second[5:]:
+                copy.wait_recv()
+            for index in (0, 9):
+                ym2[index] = y_merge(yr2[0, index], yr2[1, index])
+            for side, index in ((0, 0), (1, 9)):
+                s01[index, 0:8, :] = exz_r[side]
+                s01[index, 56:64, :] = exz_r[side]
+            ready = range(CHUNK_TILES * (chunk + 1) - 1)
+            lax.fori_loop(0, 4, lambda j, carry: lighthill(lax.rem(j + 6, 8), ready), 0)
     send_wave(True)
-    for copy in second[5:]:
-        copy.wait_recv()
-    for index in (0, 9):
-        ym2[index] = y_merge(yr2[0, index], yr2[1, index])
-    for side, index in ((0, 0), (1, 9)):
-        s01[index, 0:8, :] = exz_r[side]
-        s01[index, 56:64, :] = exz_r[side]
-    lax.fori_loop(0, 4, lambda j, carry: lighthill(lax.rem(j + 6, 8), carry), 0)
+    late = range(CHUNK_TILES * (CHUNKS - 1) - 1, ZT)
+    lax.fori_loop(0, 4, lambda j, carry: lighthill(lax.rem(j + 6, 8), late), 0)
 
     pieces = []
     for zp in range(12):

time: 46.1 us -> 47 us (1.020)
    pallas_call x1, Pallas kernels: 44.3 us -> 44.8 us  [on_device(): pl.pallas_call(functools.partial(kernel, sizes, far_order), out_shape=(vm...]
where the time goes in v6:
time: 47 us; the launch traced here: 46.4 us
  Pallas kernels  45.7 us (97%)
  between operations  0.64 us (1%)
    pallas_call x1, Pallas kernels, on_device(): pl.pallas_call(functools.partial(kernel, sizes, far_order), out_shape=(vm...  44.8 us
    pallas_call x1, Pallas kernels, on_device(): pl.pallas_call(hand_on, out_shape=tuple((jax.ShapeDtypeStruct(r.shape, f3...  0.99 us

profile of v6, /device:TPU:1, one launch (start us, length us, event | category | flops | bytes accessed | tf_op | source)
XLA Modules:
  0.0 46.4 jit_solution(1533795546613154509)
XLA Ops:
  0.6 44.8 %jet_step.1 = (f32[5,8,48,128]{3,2,1,0:T(8,128)S(1)}, f32[3,8,128]{2,1,0:T(8,128)S(1)}) custom-call(f32[5,8,48,128]{3,2,1,0:T(8,128)} %les_ref.1, f32[3,8,128]{2,1,0:T(8,128)} %wave_in.1, bf16[6144,128]{1,0:T(8,128)(2,1)} %bitcast.4, s32[1,4,8]{2,1,0:T(4,128)} %bitcast.5, s32[1,4,8]{2,1,0:T(4,128)} %bitcast.6, s32[1,4,8]{2,1,0:T(4,128)} %bitcast.7, ...), custom_call_target="tpu_custom_call" | custom-call | tf_op jit(solution)/shard_map/jet_step/pallas_call | solution.py:648
  45.4 1.0 %hand_on.1 = (f32[5,8,48,128]{3,2,1,0:T(8,128)}, f32[3,8,128]{2,1,0:T(8,128)}) custom-call(f32[5,8,48,128]{3,2,1,0:T(8,128)S(1)} %get-tuple-element.4.les_in, f32[3,8,128]{2,1,0:T(8,128)S(1)} %get-tuple-element.5.wave_in), custom_call_target="tpu_custom_call" | custom-call | tf_op jit(solution)/shard_map/hand_on/pallas_call | solution.py:657

commit v7 on v5

--- a/solution.py
+++ b/solution.py
@@ -580,6 +580,10 @@
     now = [assemble(wave_block(f)) for f in range(3)]
     no_source = jnp.zeros((24, 256), jnp.float32)
     opening = wave_rates(now, no_source, inverse_radius)
+    for copy in sum(x_first + x_second, first + second):
+        copy.wait_send()
+    pltpu.make_async_copy(others, others, all_send.at[0]).wait()
+    pltpu.make_async_copy(near_wave, near_wave, wave_send.at[0]).wait()
     pltpu.make_async_copy(near_source, near_source, src_recv.at[0]).wait()
     beside = jnp.where(wide_lane[:, 0:128] < 64, near_source[1], near_source[0])
     source = jnp.concatenate([own_source[...], beside], axis=1) * inside
@@ -594,10 +598,6 @@
     for f in range(3):
         wave_out[f] = now[f][8:16, 0:128]
 
-    for copy in sum(x_first + x_second, first + second):
-        copy.wait_send()
-    pltpu.make_async_copy(others, others, all_send.at[0]).wait()
-    pltpu.make_async_copy(near_wave, near_wave, wave_send.at[0]).wait()
     pltpu.make_async_copy(near_source, near_source, src_send.at[0]).wait()
 
 

time: 46.1 us -> 46 us (level)
  no operation moved by 1% of the time
where the time goes in v7:
time: 46 us; the launch traced here: 45.9 us
  Pallas kernels  45.2 us (98%)
  between operations  0.64 us (1%)
    pallas_call x1, Pallas kernels, on_device(): pl.pallas_call(functools.partial(kernel, sizes, far_order), out_shape=(vm...  44.2 us
    pallas_call x1, Pallas kernels, on_device(): pl.pallas_call(hand_on, out_shape=tuple((jax.ShapeDtypeStruct(r.shape, f3...  0.99 us

profile of v7, /device:TPU:1, one launch (start us, length us, event | category | flops | bytes accessed | tf_op | source)
XLA Modules:
  0.0 45.9 jit_solution(16791155666176404614)
XLA Ops:
  0.6 44.2 %jet_step.1 = (f32[5,8,48,128]{3,2,1,0:T(8,128)S(1)}, f32[3,8,128]{2,1,0:T(8,128)S(1)}) custom-call(f32[5,8,48,128]{3,2,1,0:T(8,128)} %les_ref.1, f32[3,8,128]{2,1,0:T(8,128)} %wave_in.1, bf16[6144,128]{1,0:T(8,128)(2,1)} %bitcast.4, s32[1,4,8]{2,1,0:T(4,128)} %bitcast.5, s32[1,4,8]{2,1,0:T(4,128)} %bitcast.6, s32[1,4,8]{2,1,0:T(4,128)} %bitcast.7, ...), custom_call_target="tpu_custom_call" | custom-call | tf_op jit(solution)/shard_map/jet_step/pallas_call | solution.py:642
  44.9 1.0 %hand_on.1 = (f32[5,8,48,128]{3,2,1,0:T(8,128)}, f32[3,8,128]{2,1,0:T(8,128)}) custom-call(f32[5,8,48,128]{3,2,1,0:T(8,128)S(1)} %get-tuple-element.4.les_in, f32[3,8,128]{2,1,0:T(8,128)S(1)} %get-tuple-element.5.wave_in), custom_call_target="tpu_custom_call" | custom-call | tf_op jit(solution)/shard_map/hand_on/pallas_call | solution.py:651
